TPU v7x, 128 devices: a whole 4x4x4 slice. The times are simulated.
128 devices in a mesh: dp: 8 (over z_lo, y), sp: 16 (over x, z_hi, core).
Axes of the slice: x: 4, y: 4, z: 4 (z_hi: 2, z_lo: 2; z = z_hi * 2 + z_lo), core: 2. Of those that a mesh axis runs over, the one named last changes fastest.
Arguments:
- feats: bfloat16 [8, 32, 256, 128], P('dp', None, 'sp'), may hold values from -62 to 62
- conv_w: bfloat16 [1152, 256], replicated, may hold values from -0.1875 to 0.1875
- group_norm_gain: float32 [256], replicated, may hold values from 0.5 to 1.5
- group_norm_bias: float32 [256], replicated, may hold values from -3 to 3
- emb_w: bfloat16 [256, 3072], replicated, may hold values from -0.375 to 0.375
- time_w: bfloat16 [256, 9216], replicated, may hold values from -0.375 to 0.375
- up_w: bfloat16 [3072, 6144], P(None, 'sp'), may hold values from -0.109375 to 0.109375
- down_w: bfloat16 [6144, 3072], P('sp'), may hold values from -0.078125 to 0.078125
- steps: int32 [8], P('dp'), may hold values from 0 to 999
- cotangent: bfloat16 [8, 2048, 3072], P('dp', 'sp'), may hold values from -28 to 28
Outputs:
- grad_conv: float32 [1152, 256], replicated
- grad_up: float32 [3072, 6144], P('dp', 'sp')
- grad_down: float32 [6144, 3072], P('sp', 'dp')
All inputs are finite; a program needn't handle non-finite values.
Results may differ from a plain program's by a relative error of at most 0.012.
Values may be sent and summed in bfloat16 or wider, within the bound.
A program may use at most 192 MiB of HBM per device.

v0:
```python
import math

import jax
import jax.numpy as jnp
from jax import lax
from jax.sharding import Mesh
from jax.sharding import PartitionSpec as P

NORM_GROUPS = 32
SP = ("sp_0", "sp_1", "sp_2")
DP_SP = ("dp", "sp_0", "sp_1", "sp_2")


def from_behind(array, axis, by):
    length = lax.axis_size(axis)
    pairs = [(i, i + by) for i in range(length) if 0 <= i + by < length]
    return lax.ppermute(array, axis, pairs)


def copy_for_each(array, axis):
    length = lax.axis_size(axis)
    return lax.all_to_all(
        jnp.broadcast_to(array[None], (length, *array.shape)), axis, 0, 0, tiled=True
    )


def over_copies(array, axis):
    return copy_for_each(array, axis).sum(axis=0)


def in_one(arrays, axis):
    ends = [0]
    for a in arrays:
        ends.append(ends[-1] + a.size)
    subtotal = over_copies(jnp.concatenate([a.ravel() for a in arrays]), axis)
    return tuple((subtotal[b:e].reshape(a.shape) for a, b, e in zip(arrays, ends, ends[1:])))


def side_by_side(arrays, axis, dim, along):
    both = jnp.concatenate(arrays, axis=along)
    filled, at, finished = (lax.all_gather(both, axis, axis=dim, tiled=True), 0, [])
    for a in arrays:
        finished.append(lax.slice_in_dim(filled, at, at + a.shape[along], axis=along))
        at += a.shape[along]
    return tuple(finished)


def in_blocks(array, dim, length):
    before, after = (array.shape[:dim], array.shape[dim + 1 :])
    return jnp.moveaxis(array.reshape(*before, length, -1, *after), dim, 0)


def sum_by_chip(array, chips, core, dim):
    sizes = (lax.axis_size(chips), lax.axis_size(core))
    parts = in_blocks(array, dim, sizes[0] * sizes[1])
    inside = parts.shape[1:]
    parts = parts.reshape(*sizes, *inside).swapaxes(0, 1).reshape(-1, *inside)
    parts = lax.psum_scatter(parts, core, scatter_dimension=0, tiled=True)
    return lax.psum_scatter(parts, chips, scatter_dimension=0, tiled=True)[0]


def sum_packed(arrays, axis, dims):
    length = lax.axis_size(axis)
    parts = [in_blocks(a, dim, length) for a, dim in zip(arrays, dims)]
    lines = jnp.concatenate([b.reshape(length, -1) for b in parts], axis=1)
    rows = max(16, -(-lines.shape[1] // 1024) * 8)
    lines = jnp.pad(lines, ((0, 0), (0, rows * 128 - lines.shape[1]))).reshape(-1, 128)
    ravelled, at, finished = (lax.psum_scatter(lines, axis, tiled=True).reshape(-1), 0, [])
    for b in parts:
        part = b[0]
        finished.append(ravelled[at : at + part.size].reshape(part.shape))
        at += part.size
    return tuple(finished)


def gelu_pair(u):
    coef = math.sqrt(2.0 / math.pi)
    inner = coef * (u + 0.044715 * u * u * u)
    tangent = jnp.tanh(inner)
    value = 0.5 * u * (1.0 + tangent)
    slope = 0.5 * (1.0 + tangent) + 0.5 * u * (1.0 - tangent * tangent) * coef * (
        1.0 + 3.0 * 0.044715 * u * u
    )
    return (value, slope)


def silu_pair(value):
    sigma = jax.nn.sigmoid(value)
    return (value * sigma, sigma * (1.0 + value * (1.0 - sigma)))


def modulation(step_value, time_w):
    half = time_w.shape[0] // 2
    freqs = jnp.exp(-math.log(10000.0) * jnp.arange(half, dtype=jnp.float32) / half)
    angle = step_value.astype(jnp.float32) * freqs
    embed = jnp.concatenate([jnp.cos(angle), jnp.sin(angle)])
    mixed = jnp.dot(
        jax.nn.silu(embed).astype(jnp.bfloat16)[None, :], time_w, preferred_element_type=jnp.float32
    )[0]
    width = time_w.shape[1] // 3
    return (mixed[:width], mixed[width : 2 * width], mixed[2 * width :])


def make_patches(padded, rows, cols):
    pieces = []
    for row_tap in range(3):
        for col_tap in range(3):
            pieces.append(
                padded[row_tap : row_tap + 2 * rows : 2, col_tap : col_tap + 2 * cols : 2, :]
            )
    stacked = jnp.concatenate(pieces, axis=-1)
    return stacked.reshape(rows * cols, stacked.shape[-1])


def group_totals(first, second, groups):
    tokens, width = first.shape
    first_g = first.reshape(tokens, groups, width // groups)
    second_g = second.reshape(tokens, groups, width // groups)
    return (jnp.sum(first_g, axis=(0, 2)), jnp.sum(second_g, axis=(0, 2)))


def broadcast_groups(values, width):
    return jnp.repeat(values, width // values.shape[0])


def contract(left, right, left_dim, right_dim):
    return lax.dot_general(
        left, right, (((left_dim,), (right_dim,)), ((), ())), preferred_element_type=jnp.float32
    )


def on_device(
    feats, conv_w, group_norm_gain, group_norm_bias, emb_w, time_w, up_w, down_w, steps, cotangent
):
    devices_sp = lax.axis_size(SP)
    image = feats[0]
    rows_in, cols_in, _ = image.shape
    rows = rows_in // 2
    cols = cols_in // 2
    seq_rows = rows // devices_sp
    channel_count = conv_w.shape[1]
    rim = from_behind(image[:, cols_in - 1, :], SP, 1)
    widened = jnp.concatenate([rim[:, None, :], image], axis=1)
    padded = jnp.pad(widened, ((1, 0), (0, 0), (0, 0)))
    patches = make_patches(padded, rows, cols)
    normed_value = jnp.dot(patches, conv_w, preferred_element_type=jnp.float32)
    first, second = group_totals(normed_value, normed_value * normed_value, NORM_GROUPS)
    first, second = in_one((first, second), SP)
    group_count = normed_value.shape[0] * devices_sp * (channel_count // NORM_GROUPS)
    group_mean = first / group_count
    rstd = lax.rsqrt(second / group_count - group_mean * group_mean + 1e-05)
    channel_rstd = broadcast_groups(rstd, channel_count)
    centered_input = (normed_value - broadcast_groups(group_mean, channel_count)) * channel_rstd
    preactivation = centered_input * group_norm_gain + group_norm_bias
    act_val, silu_slope = silu_pair(preactivation)
    act_b = act_val.astype(jnp.bfloat16)
    shift, scale, gate = modulation(steps[0], time_w)
    cot_seq = cotangent[0]
    moved = lax.all_to_all(
        act_b.reshape(rows, cols, channel_count), SP, split_axis=0, concat_axis=1, tiled=True
    )
    local_act = moved.reshape(seq_rows * cols * devices_sp, channel_count)
    hidden_in = jnp.dot(local_act, emb_w, preferred_element_type=jnp.float32)
    centered = hidden_in - jnp.mean(hidden_in, axis=-1, keepdims=True)
    token_rstd = lax.rsqrt(jnp.mean(centered * centered, axis=-1, keepdims=True) + 1e-06)
    hhat = centered * token_rstd
    normed = (hhat * (1.0 + scale) + shift).astype(jnp.bfloat16)
    all_normed, all_cot = side_by_side((normed, cot_seq), SP, 0, 1)
    upper = jnp.dot(all_normed, up_w, preferred_element_type=jnp.float32)
    gelu_val, gelu_slope = gelu_pair(upper)
    hid = gelu_val.astype(jnp.bfloat16)
    scaled_cot = (all_cot.astype(jnp.float32) * gate).astype(jnp.bfloat16)
    dhid = contract(scaled_cot, down_w, 1, 1)
    dupper = (dhid * gelu_slope).astype(jnp.bfloat16)
    dnormed = sum_by_chip(
        contract(dupper, up_w, 1, 1).astype(jnp.bfloat16), ("sp_0", "sp_1"), "sp_2", 0
    ).astype(jnp.float32)
    grad_up_local = contract(all_normed, dupper, 0, 0)
    grad_down_local = contract(hid, scaled_cot, 0, 0)
    grad_up, grad_down = tuple(
        (
            part.astype(jnp.float32)
            for part in sum_packed(
                (grad_up_local.astype(jnp.bfloat16), grad_down_local.astype(jnp.bfloat16)),
                "dp",
                (0, 1),
            )
        )
    )
    dhh = dnormed * (1.0 + scale)
    dhh_mean = jnp.mean(dhh, axis=-1, keepdims=True)
    dhh_cross = jnp.mean(dhh * hhat, axis=-1, keepdims=True)
    dh_val = (
        cot_seq.astype(jnp.float32) + token_rstd * (dhh - dhh_mean - hhat * dhh_cross)
    ).astype(jnp.bfloat16)
    dact = contract(dh_val, emb_w, 1, 1)
    back_tiles = lax.all_to_all(
        dact.reshape(seq_rows, cols * devices_sp, channel_count).astype(jnp.bfloat16),
        SP,
        split_axis=1,
        concat_axis=0,
        tiled=True,
    ).astype(jnp.float32)
    dact_tile = back_tiles.reshape(rows * cols, channel_count)
    input_gradient = dact_tile * silu_slope * group_norm_gain
    backward_first, backward_second = group_totals(
        input_gradient, input_gradient * centered_input, NORM_GROUPS
    )
    backward_first, backward_second = in_one((backward_first, backward_second), SP)
    normed_gradient = (
        channel_rstd
        * (
            input_gradient
            - broadcast_groups(backward_first / group_count, channel_count)
            - centered_input * broadcast_groups(backward_second / group_count, channel_count)
        )
    ).astype(jnp.bfloat16)
    conv_local = contract(patches, normed_gradient, 0, 0)
    grad_conv = lax.psum(conv_local, DP_SP)
    return (grad_conv, grad_up, grad_down)


def solution(mesh):
    finer = Mesh(mesh.devices.reshape(mesh.shape["dp"], 4, 2, 2), ("dp", "sp_0", "sp_1", "sp_2"))
    in_specs = (
        P("dp", None, SP, None),
        P(),
        P(),
        P(),
        P(),
        P(),
        P(None, SP),
        P(SP, None),
        P("dp"),
        P("dp", SP, None),
    )
    out_specs = (P(), P("dp", SP), P(SP, "dp"))
    return jax.shard_map(
        on_device, mesh=finer, in_specs=in_specs, out_specs=out_specs, check_vma=False
    )
```

profile of v0, /device:TPU:1, one launch (start us, length us, event | category | flops | bytes accessed | tf_op | source)
XLA Modules:
  0.0 589.0 jit_solution(9743201290991420241)
XLA Ops:
  7.2 1.1 copy.52
  8.3 6.9 %collective-permute-start = (bf16[32,128]{1,0:T(8,128)(2,1)S(1)}, bf16[32,128]{1,0:T(8,128)(2,1)S(1)}, u32[]{:S(2)}, u32[]{:S(2)}) collective-permute-start(bf16[32,128]{1,0:T(8,128)(2,1)S(1)} %slice_bitcast_fusion), channel_id=1, source_target_pairs={{0,1},{1,2},{2,3},{3,4},{4,5},{5,6},{6,7},{7,8},{8,9},{9,10},{10,1... | collective-permute-start | bytes 24584 | tf_op jit(solution)/shard_map/ppermute | solution.py:17
  16.0 0.2 slice.74
  16.5 0.3 slice.72
  17.2 0.3 slice.69
  18.0 0.4 slice.75
  18.6 1.3 fusion.62
  20.4 0.6 broadcast_in_dim.15
  21.0 7.9 %all-to-all-start = ((f32[16,1,64]{2,1,0:T(1,128)}), f32[16,1,64]{2,1,0:T(1,128)S(1)}, u32[]{:S(2)}, u32[]{:S(2)}) async-start(f32[16,1,64]{2,1,0:T(1,128)} %broadcast_in_dim.15), calls=%async_computation | async-start | bytes 16384 | tf_op jit(solution)/shard_map/all_to_all | solution.py:22
  29.0 3.1 fusion.66
  32.0 3.9 all-to-all-done
  36.3 0.7 fusion.52
  37.0 4.0 all-to-all-start.1
  41.0 7.4 %all-to-all-done.1 = bf16[16,8,256]{2,1,0:T(8,128)(2,1)S(1)} async-done(((bf16[16,8,256]{2,1,0:T(8,128)(2,1)}), bf16[16,8,256]{2,1,0:T(8,128)(2,1)S(1)}, u32[]{:S(2)}, u32[]{:S(2)}) %all-to-all-start.1) | async-done | bytes 65568 | tf_op jit(solution)/shard_map/all_to_all | solution.py:159
  48.4 1.9 fusion.65
  50.4 0.3 multiply_reduce_fusion
  50.7 0.9 copy-done.2
  51.6 0.3 add_convert_fusion
  51.9 1.3 pad_maximum_fusion.1
  53.3 0.2 reduce-scatter.4.cloned.1.call-start
  53.5 146.6 %all-gather.2.cloned.1.call-done = bf16[2048,6144]{1,0:T(8,128)(2,1)} async-done(((bf16[128,6144]{1,0:T(8,128)(2,1)}), bf16[2048,6144]{1,0:T(8,128)(2,1)}) %all-gather.2.cloned.1.call-update) | async-done | bytes 25165840 | tf_op jit(solution)/shard_map/all_gather | solution.py:41
  200.1 9.7 %fusion.2 = f32[2048,384]{1,0:T(8,128)S(1)} fusion(bf16[3072,384]{1,0:T(8,128)(2,1)S(1)} %copy-done, bf16[2048,6144]{1,0:T(8,128)(2,1)} %all-gather.2.cloned.1.call-done), kind=kOutput, calls=%fused_computation.4 | convolution fusion | flops 4831838208 | bytes 18087936 | tf_op jit(solution)/shard_map/dot_general | solution.py:169
  209.9 12.3 %fusion.16 = bf16[2048,384]{1,0:T(8,128)(2,1)S(1)} fusion(f32[2048,384]{1,0:T(8,128)S(1)} %fusion.2, bf16[384,3072]{1,0:T(8,128)(2,1)S(1)} %copy-done.8, bf16[2048,6144]{1,0:T(8,128)(2,1)} %all-gather.2.cloned.1.call-done, f32[3072]{0:T(1024)S(1)} %get-tuple-element.12), kind=kOutput, calls=%fused_computation.19 | convolution fusion | flops 4865654784 | bytes 19673088 | tf_op jit(solution)/shard_map/dot_general | solution.py:127
  222.2 7.0 %convolution_convert_fusion = bf16[2048,3072]{1,0:T(8,128)(2,1)S(1)} fusion(bf16[2048,384]{1,0:T(8,128)(2,1)S(1)} %fusion.16, bf16[3072,384]{1,0:T(8,128)(2,1)S(1)} %copy-done), kind=kOutput, calls=%fused_computation.1 | convolution fusion | flops 4838129664 | bytes 16515072 | tf_op jit(solution)/shard_map/dot_general | solution.py:127
  229.3 5.4 copy.33
  234.6 0.3 reduce-scatter.6.cloned.1.call-start
  234.9 1.1 copy-done.10
  236.0 10.8 %fusion.7 = bf16[3072,384]{1,0:T(8,128)(2,1)} fusion(bf16[2048,384]{1,0:T(8,128)(2,1)S(1)} %copy-done.10, bf16[2048,6144]{1,0:T(8,128)(2,1)} %all-gather.2.cloned.1.call-done), kind=kOutput, calls=%fused_computation.12 | convolution fusion | flops 4833017856 | bytes 16515072 | tf_op jit(solution)/shard_map/dot_general | solution.py:127
  246.8 3.2 reshape_reshape.7
  250.0 13.4 %fusion.6 = bf16[384,3072]{1,0:T(8,128)(2,1)S(1)} fusion(bf16[2048,6144]{1,0:T(8,128)(2,1)} %all-gather.2.cloned.1.call-done, f32[3072]{0:T(1024)S(1)} %get-tuple-element.12, f32[2048,384]{1,0:T(8,128)} %copy-done.11), kind=kOutput, calls=%fused_computation.11 | convolution fusion | flops 4858970112 | bytes 18100224 | tf_op jit(solution)/shard_map/dot_general | solution.py:127
  263.4 1.9 copy.37
  265.4 0.3 reduce-scatter.8.cloned.1.call-start
  265.7 10.4 %pad_maximum_fusion = bf16[8,294912]{1,0:T(8,128)(2,1)} fusion(bf16[8,147456]{1,0:T(8,128)(2,1)} %bitcast.67, bf16[8,147456]{1,0:T(8,128)(2,1)S(1)} %reshape_reshape.7), kind=kLoop, calls=%fused_computation.10 | loop fusion | flops 9437184 | bytes 9437184 | tf_op jit(solution)/shard_map/concatenate | solution.py:65
  276.1 6.6 %reshape.118 = bf16[18432,128]{1,0:T(8,128)(2,1)} reshape(bf16[8,294912]{1,0:T(8,128)(2,1)} %pad_maximum_fusion) | data formatting | bytes 9437184 | tf_op jit(solution)/shard_map/reshape | solution.py:67
  282.8 79.5 %reduce-scatter.6.cloned.1.call-done = bf16[1,128,3072]{2,1,0:T(8,128)(2,1)} async-done(((bf16[8,128,3072]{2,1,0:T(8,128)(2,1)}), bf16[1,128,3072]{2,1,0:T(8,128)(2,1)}) %reduce-scatter.6.cloned.1.call-update) | async-done | bytes 786448 | tf_op jit(solution)/shard_map/reduce_scatter | solution.py:59
  362.3 1.6 fusion.19
  364.0 2.5 fusion.29
  366.6 0.5 broadcast.119
  367.1 1.0 reduce.10
  368.1 12.2 %all_to_all.30 = bf16[16,2,1024]{2,1,0:T(2,128)(2,1)S(1)} all-to-all(bf16[16,2,1024]{2,1,0:T(2,128)(2,1)S(1)} %reshape.125), channel_id=1, replica_groups=mesh['dp'=8,'sp_0'=4,'sp_1'=2,'sp_2'=2] {'sp_0','sp_1','sp_2'}, dimensions={0} | all-to-all | bytes 131072 | tf_op jit(solution)/shard_map/all_to_all | solution.py:197
  381.0 10.0 %all_to_all.31 = f32[16,1,64]{2,1,0:T(1,128)S(1)} all-to-all(f32[16,1,64]{2,1,0:T(1,128)S(1)} %broadcast_in_dim.18), channel_id=1, replica_groups=mesh['dp'=8,'sp_0'=4,'sp_1'=2,'sp_2'=2] {'sp_0','sp_1','sp_2'}, dimensions={0} | all-to-all | bytes 8192 | tf_op jit(solution)/shard_map/all_to_all | solution.py:22
  391.5 1.4 fusion.38
  392.9 29.4 %reduce-scatter.8.cloned.1.call-done = bf16[2304,128]{1,0:T(8,128)(2,1)} async-done(((bf16[18432,128]{1,0:T(8,128)(2,1)}), bf16[2304,128]{1,0:T(8,128)(2,1)}) %reduce-scatter.8.cloned.1.call-update) | async-done | bytes 589840 | tf_op jit(solution)/shard_map/reduce_scatter | solution.py:68
  422.3 1.1 slice_convert_fusion
  423.4 1.0 reshape.122
  424.4 1.0 reshape.121
  425.3 154.8 %all-reduce.3.cloned.1.call-done = f32[1152,256]{1,0:T(8,128)} async-done(((f32[1152,256]{1,0:T(8,128)}), f32[1152,256]{1,0:T(8,128)}) %all-reduce.3.cloned.1.call-update) | async-done | bytes 1179664 | tf_op jit(solution)/shard_map/psum | solution.py:219
  580.2 2.4 copy.64
  (82 shorter events, 3.6 us)
Async XLA Ops:
  7.2 193.0 %copy-start = (bf16[3072,384]{1,0:T(8,128)(2,1)S(1)}, bf16[3072,384]{1,0:T(8,128)(2,1)}, u32[]{:S(2)}) copy-start(bf16[3072,384]{1,0:T(8,128)(2,1)} %param.16) | copy-start | bytes 7077892
  8.3 7.7 %collective-permute-start = (bf16[32,128]{1,0:T(8,128)(2,1)S(1)}, bf16[32,128]{1,0:T(8,128)(2,1)S(1)}, u32[]{:S(2)}, u32[]{:S(2)}) collective-permute-start(bf16[32,128]{1,0:T(8,128)(2,1)S(1)} %slice_bitcast_fusion), channel_id=1, source_target_pairs={{0,1},{1,2},{2,3},{3,4},{4,5},{5,6},{6,7},{7,8},{8,9},{9,10},{10,1... | collective-permute-start | bytes 24584 | tf_op jit(solution)/shard_map/ppermute | solution.py:17
  18.5 17.8 %copy-start.6 = (f32[256]{0:T(256)S(1)}, f32[256]{0:T(256)}, u32[]{:S(2)}) copy-start(f32[256]{0:T(256)} %param.13) | copy-start | bytes 3076
  18.5 17.8 %copy-start.7 = (f32[256]{0:T(256)S(1)}, f32[256]{0:T(256)}, u32[]{:S(2)}) copy-start(f32[256]{0:T(256)} %param.12) | copy-start | bytes 3076
  21.0 14.8 %all-to-all-start = ((f32[16,1,64]{2,1,0:T(1,128)}), f32[16,1,64]{2,1,0:T(1,128)S(1)}, u32[]{:S(2)}, u32[]{:S(2)}) async-start(f32[16,1,64]{2,1,0:T(1,128)} %broadcast_in_dim.15), calls=%async_computation | async-start | bytes 16384 | tf_op jit(solution)/shard_map/all_to_all | solution.py:22
  37.0 11.4 %all-to-all-start.1 = ((bf16[16,8,256]{2,1,0:T(8,128)(2,1)}), bf16[16,8,256]{2,1,0:T(8,128)(2,1)S(1)}, u32[]{:S(2)}, u32[]{:S(2)}) async-start(bf16[16,8,256]{2,1,0:T(8,128)(2,1)} %fusion.52), calls=%async_computation.1 | async-start | bytes 131072 | tf_op jit(solution)/shard_map/all_to_all | solution.py:159
  41.0 159.2 %all-gather.2.cloned.1.call-start = ((), (), s32[]{:S(2)}) async-start(), calls=%async_computation.7 | async-start | bytes 26738688 | tf_op jit(solution)/shard_map/all_gather | solution.py:41
  48.4 3.5 copy-start.4
  50.4 1.2 copy-start.2
  53.3 212.1 %reduce-scatter.4.cloned.1.call-start = ((), (), s32[]{:S(2)}) async-start(), calls=%async_computation.8 | async-start | bytes 18874368 | tf_op jit(solution)/shard_map/reduce_scatter | solution.py:58
  200.1 9.8 %copy-start.8 = (bf16[384,3072]{1,0:T(8,128)(2,1)S(1)}, bf16[384,3072]{1,0:T(8,128)(2,1)}, u32[]{:S(2)}) copy-start(bf16[384,3072]{1,0:T(8,128)(2,1)} %param.17) | copy-start | bytes 7077892
  209.9 12.3 %copy-start.11 = (f32[2048,384]{1,0:T(8,128)}, f32[2048,384]{1,0:T(8,128)S(1)}, u32[]{:S(2)}) copy-start(f32[2048,384]{1,0:T(8,128)S(1)} %fusion.2) | copy-start | bytes 9437188
  222.2 7.0 %copy-start.9 = (bf16[2048,384]{1,0:T(8,128)(2,1)}, bf16[2048,384]{1,0:T(8,128)(2,1)S(1)}, u32[]{:S(2)}) copy-start(bf16[2048,384]{1,0:T(8,128)(2,1)S(1)} %fusion.16) | copy-start | bytes 4718596
  234.6 1.4 copy-start.10
  234.6 127.7 %reduce-scatter.6.cloned.1.call-start = ((), (), s32[]{:S(2)}) async-start(), calls=%async_computation.9 | async-start | bytes 7077888 | tf_op jit(solution)/shard_map/reduce_scatter | solution.py:59
  265.4 156.9 %reduce-scatter.8.cloned.1.call-start = ((), (), s32[]{:S(2)}) async-start(), calls=%async_computation.11 | async-start | bytes 5308416 | tf_op jit(solution)/shard_map/reduce_scatter | solution.py:68
  282.7 79.6 %copy-start.3 = (f32[128,3072]{1,0:T(8,128)S(1)}, f32[128,3072]{1,0:T(8,128)}, u32[]{:S(2)}) copy-start(f32[128,3072]{1,0:T(8,128)} %copy-done.2) | copy-start | bytes 4718596
  282.7 81.2 %copy-start.5 = (bf16[1,128,3072]{2,1,0:T(8,128)(2,1)S(1)}, bf16[1,128,3072]{2,1,0:T(8,128)(2,1)}, u32[]{:S(2)}) copy-start(bf16[1,128,3072]{2,1,0:T(8,128)(2,1)} %param.19) | copy-start | bytes 2359300
  282.7 297.4 %all-reduce.3.cloned.1.call-start = ((), (), s32[]{:S(2)}) async-start(), calls=%async_computation.10 | async-start | bytes 2359296 | tf_op jit(solution)/shard_map/psum | solution.py:219
  392.8 189.7 %copy-start.1 = (bf16[3072,384]{1,0:T(8,128)(2,1)S(1)}, bf16[3072,384]{1,0:T(8,128)(2,1)}, u32[]{:S(2)}) copy-start(bf16[3072,384]{1,0:T(8,128)(2,1)} %param.16) | copy-start | bytes 7077892
Sparse Core Ops, SparseCore 0:
  53.4 146.6 all-gather.1
  234.8 21.5 reduce-scatter.3
  265.5 96.7 reduce-scatter.5
  364.7 57.5 reduce-scatter.7
  428.2 151.9 all-reduce.2
where the time goes:
time: 590 us; the launch traced here: 589 us
  waiting for transfers between devices  422 us (72%)
  matrix products  63.3 us (11%)
  local copies, waits for them, and re-layouts  29.3 us (5%)
  blocking collectives  22.2 us (4%)
  starting transfers between devices  19.6 us (3%)
  other arithmetic  17.9 us (3%)
  between operations  14.8 us (3%)
    psum x1, waiting for transfers between devices, on_device(): grad_conv = lax.psum(conv_local, DP_SP)  155 us
    all_gather x1, waiting for transfers between devices, side_by_side(): lax.all_gather(both, axis, axis=dim, tiled=True)  147 us
    reduce_scatter x1, waiting for transfers between devices, sum_by_chip(): return lax.psum_scatter(parts, chips, scatter_dimension=0, tiled=True)[0]  79.5 us
    dot_general x6, matrix products, contract(): lax.dot_general(left, right, (((left_dim,), (right_dim,)), ((), ())), pre...  47.3 us
    reduce_scatter x1, waiting for transfers between devices, sum_packed(): lax.psum_scatter(lines, axis, tiled=True).reshape(-1)  29.4 us
    all_to_all x1, blocking collectives, on_device(): lax.all_to_all(dact.reshape(seq_rows, cols * devices_sp, channel_count).a...  12.2 us
  transfers between devices with their start and end apart: 8, of which 6 were waited for; matrix products, arithmetic and copies ran while one was open for 10% of the time, Pallas kernels for 0%

commit v1 on v0

--- a/solution.py
+++ b/solution.py
@@ -34,15 +34,6 @@
         ends.append(ends[-1] + a.size)
     subtotal = over_copies(jnp.concatenate([a.ravel() for a in arrays]), axis)
     return tuple((subtotal[b:e].reshape(a.shape) for a, b, e in zip(arrays, ends, ends[1:])))
-
-
-def side_by_side(arrays, axis, dim, along):
-    both = jnp.concatenate(arrays, axis=along)
-    filled, at, finished = (lax.all_gather(both, axis, axis=dim, tiled=True), 0, [])
-    for a in arrays:
-        finished.append(lax.slice_in_dim(filled, at, at + a.shape[along], axis=along))
-        at += a.shape[along]
-    return tuple(finished)
 
 
 def in_blocks(array, dim, length):
@@ -156,44 +147,55 @@
     act_b = act_val.astype(jnp.bfloat16)
     shift, scale, gate = modulation(steps[0], time_w)
     cot_seq = cotangent[0]
-    moved = lax.all_to_all(
-        act_b.reshape(rows, cols, channel_count), SP, split_axis=0, concat_axis=1, tiled=True
-    )
-    local_act = moved.reshape(seq_rows * cols * devices_sp, channel_count)
-    hidden_in = jnp.dot(local_act, emb_w, preferred_element_type=jnp.float32)
-    centered = hidden_in - jnp.mean(hidden_in, axis=-1, keepdims=True)
-    token_rstd = lax.rsqrt(jnp.mean(centered * centered, axis=-1, keepdims=True) + 1e-06)
-    hhat = centered * token_rstd
-    normed = (hhat * (1.0 + scale) + shift).astype(jnp.bfloat16)
-    all_normed, all_cot = side_by_side((normed, cot_seq), SP, 0, 1)
-    upper = jnp.dot(all_normed, up_w, preferred_element_type=jnp.float32)
-    gelu_val, gelu_slope = gelu_pair(upper)
+    width = emb_w.shape[1]
+    all_cot = lax.all_gather(cot_seq, SP, axis=0, tiled=True)
+    all_act = lax.all_gather(act_b.reshape(rows, cols, channel_count), SP, axis=1, tiled=True)
+    all_act = all_act.reshape(rows * cols * devices_sp, channel_count)
+    emb_f = emb_w.astype(jnp.float32)
+    emb_mean = jnp.mean(emb_f, axis=1, keepdims=True)
+    gram = contract(emb_w, emb_w, 1, 1) - width * emb_mean * emb_mean.T
+    gram_hi = gram.astype(jnp.bfloat16)
+    gram_lo = (gram - gram_hi.astype(jnp.float32)).astype(jnp.bfloat16)
+    emb_c = emb_f - emb_mean
+    mixer = jnp.dot(
+        (emb_c * (1.0 + scale)).astype(jnp.bfloat16), up_w, preferred_element_type=jnp.float32
+    ).astype(jnp.bfloat16)
+    shift_hi = shift.astype(jnp.bfloat16)
+    shift_lo = (shift - shift_hi.astype(jnp.float32)).astype(jnp.bfloat16)
+    offset = jnp.dot(
+        jnp.stack([shift_hi, shift_lo]), up_w, preferred_element_type=jnp.float32
+    ).sum(axis=0)
+    act_gram = jnp.dot(all_act, gram_hi, preferred_element_type=jnp.float32) + jnp.dot(
+        all_act, gram_lo, preferred_element_type=jnp.float32
+    )
+    token_var = jnp.sum(all_act.astype(jnp.float32) * act_gram, axis=-1, keepdims=True) / width
+    token_rstd = lax.rsqrt(token_var + 1e-06)
+    moved = token_rstd * jnp.dot(all_act, mixer, preferred_element_type=jnp.float32)
+    gelu_val, gelu_slope = gelu_pair(moved + offset)
     hid = gelu_val.astype(jnp.bfloat16)
-    scaled_cot = (all_cot.astype(jnp.float32) * gate).astype(jnp.bfloat16)
-    dhid = contract(scaled_cot, down_w, 1, 1)
-    dupper = (dhid * gelu_slope).astype(jnp.bfloat16)
-    dnormed = sum_by_chip(
-        contract(dupper, up_w, 1, 1).astype(jnp.bfloat16), ("sp_0", "sp_1"), "sp_2", 0
-    ).astype(jnp.float32)
-    grad_up_local = contract(all_normed, dupper, 0, 0)
-    grad_down_local = contract(hid, scaled_cot, 0, 0)
-    grad_up, grad_down = tuple(
-        (
-            part.astype(jnp.float32)
-            for part in sum_packed(
-                (grad_up_local.astype(jnp.bfloat16), grad_down_local.astype(jnp.bfloat16)),
-                "dp",
-                (0, 1),
-            )
-        )
-    )
-    dhh = dnormed * (1.0 + scale)
-    dhh_mean = jnp.mean(dhh, axis=-1, keepdims=True)
-    dhh_cross = jnp.mean(dhh * hhat, axis=-1, keepdims=True)
-    dh_val = (
-        cot_seq.astype(jnp.float32) + token_rstd * (dhh - dhh_mean - hhat * dhh_cross)
-    ).astype(jnp.bfloat16)
-    dact = contract(dh_val, emb_w, 1, 1)
+    dhid = contract(all_cot, (down_w.astype(jnp.float32) * gate).astype(jnp.bfloat16), 1, 1)
+    dupper = dhid * gelu_slope
+    dupper_sum = jnp.sum(dupper, axis=0)
+    dupper_r = (dupper * token_rstd).astype(jnp.bfloat16)
+    cross = jnp.sum(dupper_r.astype(jnp.float32) * moved, axis=-1, keepdims=True)
+    part = contract(dupper_r, mixer, 1, 1) - cross * token_rstd * act_gram / width
+    dact = sum_by_chip(part.astype(jnp.bfloat16), ("sp_0", "sp_1"), "sp_2", 0).astype(jnp.float32)
+    dact = dact + contract(cot_seq, emb_w, 1, 1)
+    pair = contract(all_act, dupper_r, 0, 0).astype(jnp.bfloat16)
+    grad_down_local = contract(hid, all_cot, 0, 0) * gate
+    (grad_down,) = sum_packed((grad_down_local.astype(jnp.bfloat16),), "dp", (1,))
+    grad_down = grad_down.astype(jnp.float32)
+    all_pair = lax.all_gather(pair, "dp", axis=0, tiled=True)
+    side = lax.all_gather(jnp.concatenate([1.0 + scale, shift, dupper_sum]), "dp", axis=0)
+    here = lax.axis_index("dp")
+    block = width // lax.axis_size("dp")
+    emb_here = lax.dynamic_slice_in_dim(emb_c, here * block, block, 1)
+    scale_here = lax.dynamic_slice_in_dim(side[:, :width], here * block, block, 1)
+    shift_here = lax.dynamic_slice_in_dim(side[:, width : 2 * width], here * block, block, 1)
+    left = (emb_here[None] * scale_here[:, None, :]).astype(jnp.bfloat16)
+    grad_up = contract(left.reshape(-1, block), all_pair, 0, 0) + lax.dot_general(
+        shift_here, side[:, 2 * width :], (((0,), (0,)), ((), ())), precision=lax.Precision.HIGHEST
+    )
     back_tiles = lax.all_to_all(
         dact.reshape(seq_rows, cols * devices_sp, channel_count).astype(jnp.bfloat16),
         SP,

time: 590 us -> 520 us (0.88)
  waiting for transfers between devices: 422 us -> 368 us
  blocking collectives: 22.2 us -> 38 us
  matrix products: 63.3 us -> 50.6 us
  other arithmetic: 17.9 us -> 7.73 us
  local copies, waits for them, and re-layouts: 29.3 us -> 20.8 us
    reduce_scatter x1, waiting for transfers between devices: 79.5 us -> 26.6 us  [sum_by_chip(): return lax.psum_scatter(parts, chips, scatter_dimension=0, tiled=True)[0]]
    all_gather x1 -> x3, waiting for transfers between devices: 147 us -> 120 us  [the longest x1 86 us: on_device(): all_cot = lax.all_gather(cot_seq, SP, axis=0, tiled=True)]
    all_gather x0 -> x1, blocking collectives: none -> 23.3 us  [on_device(): lax.all_gather(jnp.concatenate([1.0 + scale, shift, dupper_sum]), 'dp', a...]
    reduce_scatter x1, waiting for transfers between devices: 29.4 us -> 41.8 us  [sum_packed(): lax.psum_scatter(lines, axis, tiled=True).reshape(-1)]
    all_to_all x1 -> x0, blocking collectives: 12.2 us -> none  [on_device(): lax.all_to_all(dact.reshape(seq_rows, cols * devices_sp, channel_count).a...]
    concatenate x2 -> x1, other arithmetic: 11.8 us -> 0.01 us  [on_device(): jnp.concatenate([1.0 + scale, shift, dupper_sum])]
    dot_general x6 -> x8, matrix products: 47.3 us -> 36.1 us  [contract(): lax.dot_general(left, right, (((left_dim,), (right_dim,)), ((), ())), pre...]
    reduce_scatter x1, waiting for transfers between devices: 0.01 us -> 9 us  [sum_by_chip(): parts = lax.psum_scatter(parts, core, scatter_dimension=0, tiled=True)]
  transfers between devices with their start and end apart: 8 -> 10, of which waited for: 6 -> 10; matrix products, arithmetic and copies ran while one was open for 10% -> 11% of each run, Pallas kernels for 0% -> 0%
where the time goes in v1:
time: 520 us; the launch traced here: 519 us
  waiting for transfers between devices  368 us (71%)
  matrix products  50.6 us (10%)
  blocking collectives  38 us (7%)
  local copies, waits for them, and re-layouts  20.8 us (4%)
  starting transfers between devices  18.2 us (4%)
  between operations  15.5 us (3%)
  other arithmetic  7.73 us (1%)
    psum x1, waiting for transfers between devices, on_device(): grad_conv = lax.psum(conv_local, DP_SP)  155 us
    all_gather x1, waiting for transfers between devices, on_device(): all_cot = lax.all_gather(cot_seq, SP, axis=0, tiled=True)  86 us
    reduce_scatter x1, waiting for transfers between devices, sum_packed(): lax.psum_scatter(lines, axis, tiled=True).reshape(-1)  41.8 us
    dot_general x8, matrix products, contract(): lax.dot_general(left, right, (((left_dim,), (right_dim,)), ((), ())), pre...  36.1 us
    all_gather x1, waiting for transfers between devices, on_device(): lax.all_gather(act_b.reshape(rows, cols, channel_count), SP, axis=1, tile...  33.8 us
    reduce_scatter x1, waiting for transfers between devices, sum_by_chip(): return lax.psum_scatter(parts, chips, scatter_dimension=0, tiled=True)[0]  26.6 us
    all_gather x1, blocking collectives, on_device(): lax.all_gather(jnp.concatenate([1.0 + scale, shift, dupper_sum]), 'dp', a...  23.3 us
    all_to_all x1, blocking collectives, copy_for_each(): lax.all_to_all(jnp.broadcast_to(array[None], (length, *array.shape)), axi...  14.7 us
  transfers between devices with their start and end apart: 10, of which 10 were waited for; matrix products, arithmetic and copies ran while one was open for 11% of the time, Pallas kernels for 0%

profile of v1, /device:TPU:1, one launch (start us, length us, event | category | flops | bytes accessed | tf_op | source)
XLA Modules:
  0.0 519.2 jit_solution(354148787067696151)
XLA Ops:
  7.2 1.1 copy.69
  8.3 6.9 %collective-permute-start = (bf16[32,128]{1,0:T(8,128)(2,1)S(1)}, bf16[32,128]{1,0:T(8,128)(2,1)S(1)}, u32[]{:S(2)}, u32[]{:S(2)}) collective-permute-start(bf16[32,128]{1,0:T(8,128)(2,1)S(1)} %slice_bitcast_fusion), channel_id=1, source_target_pairs={{0,1},{1,2},{2,3},{3,4},{4,5},{5,6},{6,7},{7,8},{8,9},{9,10},{10,1... | collective-permute-start | bytes 24584 | tf_op jit(solution)/shard_map/ppermute | solution.py:17
  15.2 0.8 collective-permute-done
  18.6 0.7 copy-done.7
  19.3 1.3 fusion.62
  21.2 14.7 %all_to_all.21 = f32[16,1,64]{2,1,0:T(1,128)S(1)} all-to-all(f32[16,1,64]{2,1,0:T(1,128)S(1)} %broadcast_in_dim.15), channel_id=1, replica_groups=mesh['dp'=8,'sp_0'=4,'sp_1'=2,'sp_2'=2] {'sp_0','sp_1','sp_2'}, dimensions={0} | all-to-all | bytes 8192 | tf_op jit(solution)/shard_map/all_to_all | solution.py:22
  36.3 1.4 fusion.44
  37.8 0.7 all-gather.11.cloned.1.call-update
  39.4 3.1 fusion.65
  42.5 0.6 subtract_convert_fusion.2
  43.4 1.0 convolution_reduce_fusion
  44.4 1.3 convolution_subtract_fusion.1
  45.7 1.7 fusion.23
  47.5 33.8 %all-gather.7.cloned.1.call-done = bf16[16,128,256]{2,1,0:T(8,128)(2,1)} async-done(((bf16[16,8,256]{2,1,0:T(8,128)(2,1)}), bf16[16,128,256]{2,1,0:T(8,128)(2,1)}) %all-gather.7.cloned.1.call-update) | async-done | bytes 1048592 | tf_op jit(solution)/shard_map/all_gather | solution.py:152
  81.3 1.8 fusion.40
  83.1 1.8 multiply_reduce_fusion.1
  84.9 2.3 convolution_multiply_fusion
  87.2 86.0 %all-gather.11.cloned.1.call-done = bf16[1,2048,3072]{2,1,0:T(8,128)(2,1)} async-done(((bf16[1,128,3072]{2,1,0:T(8,128)(2,1)}), bf16[1,2048,3072]{2,1,0:T(8,128)(2,1)}) %all-gather.11.cloned.1.call-update) | async-done | bytes 12582928 | tf_op jit(solution)/shard_map/all_gather | solution.py:151
  173.2 12.1 %multiply_reduce_fusion = (f32[2048]{0:T(1024)S(1)}, bf16[2048,384]{0,1:T(8,128)(2,1)S(1)}, f32[384]{0:T(512)}) fusion(f32[2048,384]{0,1:T(8,128)} %convolution_multiply_fusion, f32[2048]{0:T(1024)S(1)} %add_rsqrt_fusion, f32[384]{0:T(512)} %convolution_reduce_fusion, bf16[1,2048,3072]{2,1,0:T(8,128)(2,1)} %all-gather.11.cloned.1.call-done, ...), kind=kOutput, calls=%fused_computation.18 | convolution fusion | flops 4855035392 | bytes 19692544 | tf_op jit(solution)/shard_map/dot_general | solution.py:118
  185.3 0.9 fusion.14
  186.2 1.0 copy.43
  187.3 9.0 %reduce-scatter.4.cloned.1.call-done = bf16[8,128,256]{2,1,0:T(8,128)(2,1)} async-done(((bf16[16,128,256]{2,1,0:T(8,128)(2,1)}), bf16[8,128,256]{2,1,0:T(8,128)(2,1)}) %reduce-scatter.4.cloned.1.call-update) | async-done | bytes 524304 | tf_op jit(solution)/shard_map/reduce_scatter | solution.py:49
  196.4 2.9 convolution_convert_fusion
  199.5 10.9 %multiply_convert_fusion = bf16[384,3072]{1,0:T(8,128)(2,1)S(1)} fusion(bf16[1,2048,3072]{2,1,0:T(8,128)(2,1)} %all-gather.11.cloned.1.call-done, f32[3072]{0:T(1024)S(1)} %copy-done.18, f32[2048,384]{0,1:T(8,128)} %convolution_multiply_fusion, f32[384]{0:T(512)S(1)} %copy-done.24), kind=kOutput, calls=%fused_computation.6 | convolution fusion | flops 4842061824 | bytes 18101760 | tf_op jit(solution)/shard_map/dot_general | solution.py:118
  210.5 1.7 copy.67
  212.1 5.0 reshape.113
  217.2 1.9 convert_subtract_fusion
  219.1 0.8 constant_dynamic-slice_fusion.1
  220.0 23.3 %all-gather.2 = f32[8,1,6528]{2,1,0:T(1,128)S(1)} all-gather(f32[1,1,6528]{2,1,0:T(1,128)S(1)} %reshape.119), channel_id=3, replica_groups=mesh['dp'=8,'sp_0'=4,'sp_1'=2,'sp_2'=2] {'dp'}, dimensions={0}, use_global_device_ids=true | all-gather | bytes 235008 | tf_op jit(solution)/shard_map/all_gather | solution.py:189
  243.2 26.6 %reduce-scatter.6.cloned.1.call-done = bf16[1,128,256]{2,1,0:T(8,128)(2,1)} async-done(((bf16[8,128,256]{2,1,0:T(8,128)(2,1)}), bf16[1,128,256]{2,1,0:T(8,128)(2,1)}) %reduce-scatter.6.cloned.1.call-update) | async-done | bytes 65552 | tf_op jit(solution)/shard_map/reduce_scatter | solution.py:50
  269.9 2.1 fusion.25
  272.6 1.0 reduce.10
  273.6 0.7 reshape.124
  274.3 7.2 %all-to-all-start.1 = ((bf16[16,2,1024]{2,1,0:T(2,128)(2,1)}), bf16[16,2,1024]{2,1,0:T(2,128)(2,1)S(1)}, u32[]{:S(2)}, u32[]{:S(2)}) async-start(bf16[16,2,1024]{2,1,0:T(2,128)(2,1)} %reshape.124), calls=%async_computation.3 | async-start | bytes 131072 | tf_op jit(solution)/shard_map/all_to_all | solution.py:199
  281.4 0.6 fusion.64
  282.1 7.1 %all-to-all-done.1 = bf16[16,2,1024]{2,1,0:T(2,128)(2,1)S(1)} async-done(((bf16[16,2,1024]{2,1,0:T(2,128)(2,1)}), bf16[16,2,1024]{2,1,0:T(2,128)(2,1)S(1)}, u32[]{:S(2)}, u32[]{:S(2)}) %all-to-all-start.1) | async-done | bytes 65568 | tf_op jit(solution)/shard_map/all_to_all | solution.py:199
  289.9 0.6 broadcast_in_dim.18
  290.5 3.7 all-to-all-start.2
  294.3 6.9 %all-to-all-done.2 = f32[16,1,64]{2,1,0:T(1,128)S(1)} async-done(((f32[16,1,64]{2,1,0:T(1,128)}), f32[16,1,64]{2,1,0:T(1,128)S(1)}, u32[]{:S(2)}, u32[]{:S(2)}) %all-to-all-start.2) | async-done | bytes 4128 | tf_op jit(solution)/shard_map/all_to_all | solution.py:22
  301.6 2.3 fusion.29
  304.0 1.5 multiply_convert_fusion.3
  305.5 1.4 fusion.45
  306.9 0.7 all-gather.9.cloned.1.call-done
  307.6 3.7 convolution_add_fusion.1
  311.3 41.8 %reduce-scatter.8.cloned.1.call-done = bf16[1152,128]{1,0:T(8,128)(2,1)} async-done(((bf16[9216,128]{1,0:T(8,128)(2,1)}), bf16[1152,128]{1,0:T(8,128)(2,1)}) %reduce-scatter.8.cloned.1.call-update) | async-done | bytes 294928 | tf_op jit(solution)/shard_map/reduce_scatter | solution.py:59
  353.1 1.9 reshape.116
  355.0 155.0 %all-reduce.3.cloned.1.call-done = f32[1152,256]{1,0:T(8,128)} async-done(((f32[1152,256]{1,0:T(8,128)}), f32[1152,256]{1,0:T(8,128)}) %all-reduce.3.cloned.1.call-update) | async-done | bytes 1179664 | tf_op jit(solution)/shard_map/psum | solution.py:221
  510.0 2.4 copy.81
  (122 shorter events, 6.2 us)
Async XLA Ops:
  7.2 36.3 %copy-start = (bf16[3072,384]{1,0:T(8,128)(2,1)S(1)}, bf16[3072,384]{1,0:T(8,128)(2,1)}, u32[]{:S(2)}) copy-start(bf16[3072,384]{1,0:T(8,128)(2,1)} %param.16) | copy-start | bytes 7077892
  7.2 74.1 %all-gather.7.cloned.1.call-start = ((), (), s32[]{:S(2)}) async-start(), calls=%async_computation.6 | async-start | bytes 1114112 | tf_op jit(solution)/shard_map/all_gather | solution.py:152
  8.3 7.7 %collective-permute-start = (bf16[32,128]{1,0:T(8,128)(2,1)S(1)}, bf16[32,128]{1,0:T(8,128)(2,1)S(1)}, u32[]{:S(2)}, u32[]{:S(2)}) collective-permute-start(bf16[32,128]{1,0:T(8,128)(2,1)S(1)} %slice_bitcast_fusion), channel_id=1, source_target_pairs={{0,1},{1,2},{2,3},{3,4},{4,5},{5,6},{6,7},{7,8},{8,9},{9,10},{10,1... | collective-permute-start | bytes 24584 | tf_op jit(solution)/shard_map/ppermute | solution.py:17
  18.6 0.7 copy-start.7
  36.2 7.2 %copy-start.14 = (f32[256]{0:T(256)}, f32[256]{0:T(256)S(1)}, u32[]{:S(2)}) copy-start(f32[256]{0:T(256)S(1)} %mul.219) | copy-start | bytes 3076
  36.3 7.1 %copy-start.16 = (f32[256]{0:T(256)}, f32[256]{0:T(256)S(1)}, u32[]{:S(2)}) copy-start(f32[256]{0:T(256)S(1)} %sub.53) | copy-start | bytes 3076
  37.7 135.5 %all-gather.11.cloned.1.call-start = ((), (), s32[]{:S(2)}) async-start(), calls=%async_computation.12 | async-start | bytes 13369344 | tf_op jit(solution)/shard_map/all_gather | solution.py:151
  38.5 157.8 %reduce-scatter.4.cloned.1.call-start = ((), (), s32[]{:S(2)}) async-start(), calls=%async_computation.7 | async-start | bytes 1572864 | tf_op jit(solution)/shard_map/reduce_scatter | solution.py:49
  38.5 4.6 copy-start.2
  43.1 2.7 copy-start.12
  43.4 4.1 copy-start.21
  81.2 1.8 copy-start.1
  81.3 1.8 copy-start.8
  83.1 1.9 copy-start.9
  173.2 12.1 %copy-start.3 = (f32[2048,256]{1,0:T(8,128)S(1)}, f32[2048,256]{1,0:T(8,128)}, u32[]{:S(2)}) copy-start(f32[2048,256]{1,0:T(8,128)} %get-tuple-element.24) | copy-start | bytes 6291460
  173.2 12.1 %copy-start.10 = (bf16[256,384]{1,0:T(8,128)(2,1)S(1)}, bf16[256,384]{1,0:T(8,128)(2,1)}, u32[]{:S(2)}) copy-start(bf16[256,384]{1,0:T(8,128)(2,1)} %fusion.23) | copy-start | bytes 589828
  185.3 2.0 copy-start.5
  186.2 13.3 %copy-start.18 = (f32[3072]{0:T(1024)S(1)}, f32[3072]{0:T(1024)}, u32[]{:S(2)}) copy-start(f32[3072]{0:T(1024)} %get-tuple-element.17) | copy-start | bytes 36868
  186.2 13.3 %copy-start.24 = (f32[384]{0:T(512)S(1)}, f32[384]{0:T(512)}, u32[]{:S(2)}) copy-start(f32[384]{0:T(512)} %convolution_reduce_fusion) | copy-start | bytes 4612
  187.3 82.6 %reduce-scatter.6.cloned.1.call-start = ((), (), s32[]{:S(2)}) async-start(), calls=%async_computation.8 | async-start | bytes 589824 | tf_op jit(solution)/shard_map/reduce_scatter | solution.py:50
  196.3 111.3 %all-gather.9.cloned.1.call-start = ((), (), s32[]{:S(2)}) async-start(), calls=%async_computation.10 | async-start | bytes 1769472 | tf_op jit(solution)/shard_map/all_gather | solution.py:188
  199.3 153.8 %reduce-scatter.8.cloned.1.call-start = ((), (), s32[]{:S(2)}) async-start(), calls=%async_computation.11 | async-start | bytes 2654208 | tf_op jit(solution)/shard_map/reduce_scatter | solution.py:59
  212.1 5.1 copy-start.22
  217.2 2.8 copy-start.11
  217.2 2.8 copy-start.13
  217.2 2.8 copy-start.23
  217.2 52.7 %copy-start.4 = (bf16[1,128,3072]{2,1,0:T(8,128)(2,1)S(1)}, bf16[1,128,3072]{2,1,0:T(8,128)(2,1)}, u32[]{:S(2)}) copy-start(bf16[1,128,3072]{2,1,0:T(8,128)(2,1)} %param.19) | copy-start | bytes 2359300
  219.1 70.1 %copy-start.15 = (f32[256]{0:T(256)S(1)}, f32[256]{0:T(256)}, u32[]{:S(2)}) copy-start(f32[256]{0:T(256)} %copy-done.14) | copy-start | bytes 3076
  219.1 70.1 %copy-start.17 = (f32[256]{0:T(256)S(1)}, f32[256]{0:T(256)}, u32[]{:S(2)}) copy-start(f32[256]{0:T(256)} %copy-done.16) | copy-start | bytes 3076
  219.1 70.1 %copy-start.19 = (f32[256]{0:T(256)S(1)}, f32[256]{0:T(256)}, u32[]{:S(2)}) copy-start(f32[256]{0:T(256)} %param.13) | copy-start | bytes 3076
  219.1 70.1 %copy-start.20 = (f32[256]{0:T(256)S(1)}, f32[256]{0:T(256)}, u32[]{:S(2)}) copy-start(f32[256]{0:T(256)} %param.12) | copy-start | bytes 3076
  272.0 32.0 %copy-start.6 = (f32[256,384]{1,0:T(8,128)S(1)}, f32[256,384]{1,0:T(8,128)}, u32[]{:S(2)}) copy-start(f32[256,384]{1,0:T(8,128)} %constant_dynamic-slice_fusion.1) | copy-start | bytes 1179652
  274.3 14.9 %all-to-all-start.1 = ((bf16[16,2,1024]{2,1,0:T(2,128)(2,1)}), bf16[16,2,1024]{2,1,0:T(2,128)(2,1)S(1)}, u32[]{:S(2)}, u32[]{:S(2)}) async-start(bf16[16,2,1024]{2,1,0:T(2,128)(2,1)} %reshape.124), calls=%async_computation.3 | async-start | bytes 131072 | tf_op jit(solution)/shard_map/all_to_all | solution.py:199
  290.5 10.7 %all-to-all-start.2 = ((f32[16,1,64]{2,1,0:T(1,128)}), f32[16,1,64]{2,1,0:T(1,128)S(1)}, u32[]{:S(2)}, u32[]{:S(2)}) async-start(f32[16,1,64]{2,1,0:T(1,128)} %broadcast_in_dim.18), calls=%async_computation.4 | async-start | bytes 16384 | tf_op jit(solution)/shard_map/all_to_all | solution.py:22
  294.2 215.8 %all-reduce.3.cloned.1.call-start = ((), (), s32[]{:S(2)}) async-start(), calls=%async_computation.9 | async-start | bytes 2359296 | tf_op jit(solution)/shard_map/psum | solution.py:221
Sparse Core Ops, SparseCore 0:
  37.8 43.3 all-gather.6
  83.6 89.5 all-gather.10
  187.4 8.8 reduce-scatter.3
  200.2 69.6 reduce-scatter.5
  271.4 36.1 all-gather.8
  309.9 43.1 reduce-scatter.7
  358.4 151.5 all-reduce.2

commit v2 on v0

v2 whole, which is shorter than its diff:
```python
import functools
import math

import jax
import jax.numpy as jnp
from jax import lax
from jax.experimental import pallas as pl
from jax.experimental.pallas import tpu as pltpu
from jax.sharding import PartitionSpec as P

NORM_GROUPS = 32
F32 = jnp.float32
BF16 = jnp.bfloat16
MESH = pl.DeviceIdType.MESH


def gelu_pair(u):
    coef = math.sqrt(2.0 / math.pi)
    inner = coef * (u + 0.044715 * u * u * u)
    tangent = jnp.tanh(inner)
    value = 0.5 * u * (1.0 + tangent)
    slope = 0.5 * (1.0 + tangent) + 0.5 * u * (1.0 - tangent * tangent) * coef * (
        1.0 + 3.0 * 0.044715 * u * u
    )
    return (value, slope)


def nn(left, right):
    return lax.dot_general(left, right, (((1,), (0,)), ((), ())), preferred_element_type=F32)


def nt(left, right):
    return lax.dot_general(left, right, (((1,), (1,)), ((), ())), preferred_element_type=F32)


def exact(left, right, dims):
    return lax.dot_general(
        left,
        right,
        (dims, ((), ())),
        precision=lax.Precision.HIGHEST,
        preferred_element_type=F32,
    )


def split(value):
    high = value.astype(BF16)
    return high, (value - high.astype(F32)).astype(BF16)


def rows_of(first, second, like):
    which = lax.broadcasted_iota(jnp.int32, like, 0)
    return jnp.where(which == 0, first, jnp.where(which == 1, second, 0.0))


def body(
    n_sp, n_dp, es, gain_bias, patches_in, conv_in, emb_in, time_in, up_in, down_in, cot_in,
    out_conv, out_up, out_down, s,
):
    n_chip = n_sp // 2
    width = emb_in.shape[1]
    hidden = up_in.shape[1]
    block = width // n_dp
    chans = conv_in.shape[1]
    pixels = patches_in.shape[0]
    half = pixels // 2
    taps = conv_in.shape[0] // n_sp
    me = lax.axis_index("sp")
    image = lax.axis_index("dp")
    core = lax.rem(me, 2)
    chip = me // 2
    far = lax.rem(chip, 2)
    col = chip // 2
    n_col = n_chip // 2
    east_col, west_col = lax.rem(col + 1, n_col), lax.rem(col + n_col - 1, n_col)
    over_col = lax.rem(col + 2, n_col)
    sibling = chip * 2 + 1 - core
    chip_of = lambda at, level: at * 2 + level
    dev_of = lambda which: which * 2 + core
    z_chip = chip_of(col, 1 - far)
    east, west = dev_of(chip_of(east_col, far)), dev_of(chip_of(west_col, far))
    z_peer = dev_of(z_chip)

    def send(src, dst, sems, at_send, at_recv, **where):
        return pltpu.make_async_remote_copy(
            src_ref=src, dst_ref=dst, send_sem=sems.at[0, at_send], recv_sem=sems.at[1, at_recv],
            device_id=where, device_id_type=MESH,
        )

    def others(count, first, act):
        @pl.loop(1, count)
        def _(step):
            act(lax.rem(first + step, count))

    def every(count, act):
        @pl.loop(0, count)
        def _(step):
            act(step)

    barrier = pltpu.get_barrier_semaphore()
    others(n_sp, me, lambda p: pl.semaphore_signal(barrier, 1, device_id={"sp": p}, device_id_type=MESH))
    others(n_dp, image, lambda p: pl.semaphore_signal(barrier, 1, device_id={"dp": p}, device_id_type=MESH))

    loads = {}
    for index, (name, src, dst) in enumerate(
        (
            ("patches", patches_in, s.patches),
            ("conv", conv_in, s.conv),
            ("emb", emb_in, s.emb),
            ("up", up_in, s.up),
        )
    ):
        loads[name] = pltpu.make_async_copy(src, dst, s.load.at[index])

    def cot_load(p):
        columns = pl.ds(pl.multiple_of(p * block, block), block)
        return pltpu.make_async_copy(cot_in.at[:, columns], s.cot.at[p, chip], s.load.at[8 + p])

    my_rows = pl.ds(pl.multiple_of(core * hidden, hidden), hidden)
    its_rows = pl.ds(pl.multiple_of((1 - core) * hidden, hidden), hidden)

    def down_load(p):
        columns = pl.ds(pl.multiple_of(p * block, block), block)
        return pltpu.make_async_copy(
            down_in.at[:, columns], s.gated.at[p, my_rows], s.load.at[8 + n_dp + p]
        )

    def time_load(k):
        columns = pl.ds(pl.multiple_of(k * 1024, 1024), 1024)
        slot = lax.rem(k, 2)
        return pltpu.make_async_copy(time_in.at[:, columns], s.time.at[slot], s.load.at[6 + slot])

    loads["patches"].start()
    loads["conv"].start()
    every(n_dp, lambda p: cot_load(p).start())
    every(n_dp, lambda p: down_load(p).start())
    time_load(0).start()
    for name in ("emb", "up"):
        loads[name].start()

    loads["patches"].wait()
    loads["conv"].wait()
    s.z[...] = nn(s.patches[...], s.conv[...])
    z = s.z[...]
    s.stat_tx[...] = rows_of(
        jnp.sum(z, axis=0, keepdims=True), jnp.sum(z * z, axis=0, keepdims=True), (8, chans)
    )
    s.stat_rx[me] = s.stat_tx[...]

    pl.semaphore_wait(barrier, n_sp - 1 + n_dp - 1)

    def stat_copy(p):
        return send(s.stat_tx, s.stat_rx.at[me], s.stat_sem, p, me, sp=p)

    def stat_from(p):
        return send(s.stat_tx, s.stat_rx.at[p], s.stat_sem, p, p, sp=p)

    others(n_sp, me, lambda p: stat_copy(p).start())

    every(n_dp, lambda p: cot_load(p).wait())

    def turn(q):
        return lax.rem(image + 1 + q, n_dp)

    top, low = pl.ds(0, half), pl.ds(half, half)
    routes = {
        "z": (chip, None, z_peer, z_chip),
        "e": (chip, None, east, chip_of(west_col, far)),
        "w": (chip, None, west, chip_of(east_col, far)),
        "ez": (z_chip, None, east, chip_of(west_col, 1 - far)),
        "wz": (z_chip, None, west, chip_of(east_col, 1 - far)),
        "ee": (chip_of(west_col, far), top, east, chip_of(over_col, far)),
        "ww": (chip_of(east_col, far), low, west, chip_of(over_col, far)),
        "eez": (chip_of(west_col, 1 - far), top, east, chip_of(over_col, 1 - far)),
        "wwz": (chip_of(east_col, 1 - far), low, west, chip_of(over_col, 1 - far)),
    }
    order = {name: index for index, name in enumerate(routes)}

    def cot_copy(name, p, arriving=False):
        mine, part, to, theirs = routes[name]
        which = theirs if arriving else mine
        ref = s.cot.at[p, which] if part is None else s.cot.at[p, which, part, :]
        at = order[name] * n_dp + p
        return send(ref, ref, s.cot_sem, at, at, sp=to)

    def own(q):
        p = turn(q)
        for name in ("z", "e", "w"):
            cot_copy(name, p).start()

    def relay(q):
        p = turn(q)
        for name, then in (
            ("z", ("ez", "wz")),
            ("e", ("ee",)),
            ("w", ("ww",)),
            ("ez", ("eez",)),
            ("wz", ("wwz",)),
        ):
            cot_copy(name, p, True).wait_recv()
            for onward in then:
                cot_copy(onward, p).start()

    def landed(q):
        p = turn(q)
        for name in ("ee", "ww", "eez", "wwz"):
            cot_copy(name, p, True).wait_recv()

    own(0)
    own(1)

    every(n_dp, lambda p: down_load(p).wait())
    my_down, its_down = s.gated.at[:, my_rows], s.gated.at[:, its_rows]
    down_copy = send(my_down, my_down, s.pair_sem, 0, 0, sp=sibling)
    down_copy.start()

    n_time = 3 * width // 1024

    def mod_part(k):
        @pl.when(k + 1 < n_time)
        def _():
            time_load(k + 1).start()

        columns = pl.ds(pl.multiple_of(k * 1024, 1024), 1024)
        time_load(k).wait()
        s.mod[:, columns] = nn(es[...], s.time[lax.rem(k, 2)])

    every(n_time, mod_part)

    others(n_sp, me, lambda p: stat_from(p).wait_recv())
    count = pixels * n_sp * (chans // NORM_GROUPS)
    shift_by = (chans // NORM_GROUPS).bit_length() - 1

    def group_sums(ref):
        pair = lax.broadcasted_iota(jnp.int32, (chans, chans), 0) >> shift_by
        other = lax.broadcasted_iota(jnp.int32, (chans, chans), 1) >> shift_by
        same = jnp.where(pair == other, 1.0, 0.0).astype(F32)
        totals = exact(jnp.sum(ref[...], axis=0), same, ((1,), (0,))) / count
        return totals[0:1, :], totals[1:2, :]

    mean, square = group_sums(s.stat_rx)
    rstd = lax.rsqrt(square - mean * mean + 1e-05)
    s.rstd[...] = jnp.broadcast_to(rstd, s.rstd.shape)
    xhat = (s.z[...] - mean) * rstd
    s.z[...] = xhat
    pre = xhat * gain_bias[0:1, :] + gain_bias[1:2, :]
    sigma = jax.nn.sigmoid(pre)
    s.slope0[...] = sigma * (1.0 + pre * (1.0 - sigma)) * gain_bias[0:1, :]
    act = (pre * sigma).reshape(n_chip, 2, pixels // n_sp, chans)
    for k in range(2):
        s.act_tx[k] = act[:, k].reshape(half, chans).astype(BF16)
    s.act_rx[me] = s.act_tx[core]

    def act_copy(p, source):
        return send(s.act_tx.at[lax.rem(p, 2)], s.act_rx.at[source], s.act_sem, p, source, sp=p)

    others(n_sp, me, lambda p: act_copy(p, me).start())
    own(2)
    relay(0)

    loads["emb"].wait()
    loads["up"].wait()
    ones = jnp.ones((16, width), BF16)
    mean_row = nt(ones, s.emb[...])[0:1, :] / width
    s.mean_col[...] = jnp.broadcast_to(
        jnp.mean(s.emb[...].astype(F32), axis=1, keepdims=True), s.mean_col.shape
    )
    mean_col = s.mean_col[:, 0:1]
    s.gram[...] = jnp.zeros_like(s.gram)
    s.mix[...] = jnp.zeros_like(s.mix)
    s.offset[...] = jnp.zeros_like(s.offset)
    s.skip[...] = jnp.zeros_like(s.skip)

    def fold(p):
        columns = pl.ds(pl.multiple_of(p * block, block), block)
        emb = s.emb[:, columns]
        scale = s.mod[0:1, pl.ds(pl.multiple_of(width + p * block, block), block)]
        left = ((emb.astype(F32) - mean_col) * (1.0 + scale)).astype(BF16)
        up = s.up[columns, :]
        s.mix[...] += nn(left, up)
        s.gram[...] += nt(emb, emb)
        high, low_part = split(s.mod[:, columns])
        s.offset[...] += nn(high, up) + nn(low_part, up)
        s.skip[...] += nt(s.cot[p, chip], emb)

    every(n_dp, fold)
    my_cols, its_cols = my_rows, its_rows
    s.mixer[:, my_cols] = s.mix[...].astype(BF16)
    s.offsets[:, my_cols] = s.offset[...]
    mix_copy = send(s.mixer.at[:, my_cols], s.mixer.at[:, my_cols], s.pair_sem, 1, 1, sp=sibling)
    mix_copy.start()
    off_copy = send(s.offsets.at[:, my_cols], s.offsets.at[:, my_cols], s.pair_sem, 2, 2, sp=sibling)
    off_copy.start()
    own(3)
    relay(1)

    down_from = send(its_down, its_down, s.pair_sem, 0, 0, sp=sibling)
    down_copy.wait_send()
    down_from.wait_recv()

    def gate_part(p):
        gate = s.mod[0:1, pl.ds(pl.multiple_of(2 * width + p * block, block), block)]
        s.gated[p] = (s.gated[p].astype(F32) * gate).astype(BF16)

    every(n_dp, gate_part)

    others(n_sp, me, lambda p: act_copy(p, p).wait_recv())

    def place(p):
        tile = s.act_rx[p].astype(F32).reshape(n_chip, pixels // n_sp, chans)
        s.act[:, pl.ds(pl.multiple_of(p * 8, 8), 8), :] = tile

    every(n_sp, place)
    mix_from = send(s.mixer.at[:, its_cols], s.mixer.at[:, its_cols], s.pair_sem, 1, 1, sp=sibling)
    off_from = send(s.offsets.at[:, its_cols], s.offsets.at[:, its_cols], s.pair_sem, 2, 2, sp=sibling)
    mix_from.wait_recv()
    off_from.wait_recv()
    gram_hi, gram_lo = split(s.gram[...] - width * mean_col * mean_row)
    s.gram_hi[...] = gram_hi
    s.gram_lo[...] = gram_lo

    def forward(i):
        lanes = pl.ds(pl.multiple_of(i * pixels, pixels), pixels)
        wide = s.act[i]
        narrow = wide.astype(BF16)
        spread = nn(narrow, s.gram_hi[...]) + nn(narrow, s.gram_lo[...])
        var = jnp.sum(wide * spread, axis=-1, keepdims=True) / width
        token_rstd = lax.rsqrt(var + 1e-06)
        moved = nn(narrow, s.mixer[...]) * token_rstd
        value, slope = gelu_pair(moved + s.offsets[0:1, :])
        s.hid_t[:, lanes] = value.T.astype(BF16)
        s.act_t[:, lanes] = wide.T.astype(BF16)
        s.slope[i] = slope
        s.moved[i] = moved
        s.spread[i] = spread * (token_rstd / width)
        s.token_rstd[i] = jnp.broadcast_to(token_rstd, (pixels, 128))
        s.dhid[i] = jnp.zeros_like(slope)

    every(n_chip, forward)
    s.patches_t[...] = s.patches[...].astype(F32).T.astype(BF16)

    def sib_copy(p):
        return send(s.sib_tx.at[p], s.sib_rx.at[p], s.sib_sem, p, p, sp=sibling)

    def down_out(p, source, to):
        return send(s.gd_tx.at[p], s.gd_rx.at[source], s.gd_sem, p, source, dp=to)

    def block_of(q):
        p = turn(q)
        gate = s.mod[0:1, pl.ds(pl.multiple_of(2 * width + p * block, block), block)]
        cot = s.cot[p].reshape(n_chip * pixels, block)
        s.sib_tx[p] = (nn(s.hid_t[its_rows, :], cot) * gate).astype(BF16)
        sib_copy(p).start()
        s.gd_own[lax.rem(q, 2)] = nn(s.hid_t[my_rows, :], cot) * gate

        def part(h):
            rows = pl.ds(h * (n_chip // 2), n_chip // 2)
            tokens = s.cot[p, rows].reshape(n_chip // 2 * pixels, block)
            s.dhid[rows] += nt(tokens, s.gated[p]).reshape(n_chip // 2, pixels, 2 * hidden)

        every(2, part)

    def whole(q):
        p = turn(q)
        sib_copy(p).wait_recv()
        return p, s.gd_own[lax.rem(q, 2)] + s.sib_rx[p].astype(F32)

    def hand_over(q):
        p, total = whole(q)
        s.gd_tx[p] = total.astype(BF16)
        down_out(p, image, p).start()

    @pl.loop(0, n_dp)
    def _(q):
        @pl.when(q + 4 < n_dp)
        def _():
            own(q + 4)

        @pl.when(q + 2 < n_dp)
        def _():
            relay(q + 2)

        @pl.when(q > 0)
        def _():
            hand_over(q - 1)

        landed(q)
        block_of(q)

    s.du_sum[...] = jnp.zeros_like(s.du_sum)

    def backward(i):
        grad = s.dhid[i] * s.slope[i]
        s.du_sum[0:1, :] += jnp.sum(grad, axis=0, keepdims=True)
        grad = grad * s.token_rstd[i][:, 0:1]
        cross = jnp.sum(grad * s.moved[i], axis=-1, keepdims=True)
        narrow = grad.astype(BF16)
        s.du[pl.ds(pl.multiple_of(i * pixels, pixels), pixels), :] = narrow
        s.act[i] = nt(narrow, s.mixer[...]) - cross * s.spread[i]

    every(n_chip, backward)
    s.act[chip] += s.skip[...]

    def tile_of(p):
        rows = s.act[:, pl.ds(pl.multiple_of(p * 8, 8), 8), :]
        return rows.reshape(half, chans).astype(BF16)

    def part_copy(p, source):
        return send(s.part_tx.at[p], s.part_rx.at[source], s.part_sem, p, source, sp=p)

    def part_out(p):
        s.part_tx[p] = tile_of(p)
        part_copy(p, me).start()

    others(n_sp, me, part_out)
    s.part_rx[me] = tile_of(me)

    s.pairs[...] = nn(s.act_t[...], s.du[...])
    s.pair_tx[...] = s.pairs[:, its_cols].astype(BF16)
    s.sum_tx[...] = s.du_sum[:, its_cols]
    pair_copy = send(s.pair_tx, s.pair_rx, s.pair_sem, 3, 3, sp=sibling)
    pair_copy.start()
    sum_copy = send(s.sum_tx, s.sum_rx, s.pair_sem, 4, 4, sp=sibling)
    sum_copy.start()
    _, total = whole(n_dp - 1)
    out_down[...] = total

    others(n_sp, me, lambda p: part_copy(p, p).wait_recv())
    parts = []
    for k in range(2):
        total = s.part_rx[k].astype(F32)
        for j in range(1, n_chip):
            total = total + s.part_rx[2 * j + k].astype(F32)
        parts.append(total.reshape(n_chip, 1, pixels // n_sp, chans))
    dx = jnp.concatenate(parts, axis=1).reshape(pixels, chans) * s.slope0[...]
    s.slope0[...] = dx
    s.stat2_tx[...] = rows_of(
        jnp.sum(dx, axis=0, keepdims=True), jnp.sum(dx * s.z[...], axis=0, keepdims=True), (8, chans)
    )
    s.stat2_rx[me] = s.stat2_tx[...]

    def stat2_copy(p, source):
        return send(s.stat2_tx, s.stat2_rx.at[source], s.stat2_sem, p, source, sp=p)

    others(n_sp, me, lambda p: stat2_copy(p, me).start())

    pair_copy.wait_recv()
    sum_copy.wait_recv()
    s.q_tx[...] = (s.pairs[:, my_cols] + s.pair_rx[...].astype(F32)).astype(BF16)
    s.q_rx[image] = s.q_tx[...]
    du_sum = (s.du_sum[:, my_cols] + s.sum_rx[...])[0:1, :]

    def side_of(p):
        shift = s.mod[0:1, pl.ds(pl.multiple_of(p * block, block), block)]
        scale = s.mod[0:1, pl.ds(pl.multiple_of(width + p * block, block), block)]
        which = lax.broadcasted_iota(jnp.int32, (8, block), 0)
        return jnp.where(which == 2, du_sum, rows_of(1.0 + scale, shift, (8, block)))

    def q_copy(p, source):
        return send(s.q_tx, s.q_rx.at[source], s.q_sem, p, source, dp=p)

    def side_copy(p, source):
        return send(s.side_tx.at[p], s.side_rx.at[source], s.side_sem, p, source, dp=p)

    def q_out(p):
        q_copy(p, image).start()
        s.side_tx[p] = side_of(p)
        side_copy(p, image).start()

    others(n_dp, image, q_out)
    s.side_rx[image] = side_of(image)

    others(n_sp, me, lambda p: stat2_copy(p, p).wait_recv())
    first, second = group_sums(s.stat2_rx)
    dz = (s.rstd[0:1, :] * (s.slope0[...] - first - s.z[...] * second)).astype(BF16)
    s.grad[...] = nn(s.patches_t[...], dz)

    def rows_at(k):
        return pl.ds(pl.multiple_of(k * taps, 8), taps)

    def grad_copy(p, source):
        return send(s.grad_tx.at[p], s.grad_rx.at[source], s.grad_sem, p, source, sp=p)

    def grad_out(p):
        s.grad_tx[p] = s.grad[rows_at(p), :].astype(BF16)
        grad_copy(p, me).start()

    others(n_sp, me, grad_out)
    s.grad_rx[me] = s.grad[rows_at(me), :].astype(BF16)

    others(n_dp, image, lambda p: down_out(p, p, p).wait_recv())

    def add_down(p):
        out_down[...] += s.gd_rx[p].astype(F32)

    others(n_dp, image, add_down)

    others(n_sp, me, lambda p: grad_copy(p, p).wait_recv())

    def slots(ref, n):
        total = ref[0].astype(F32)
        for j in range(1, n):
            total = total + ref[j].astype(F32)
        return total

    s.all_tx[...] = slots(s.grad_rx, n_sp).astype(BF16)
    s.all_rx[image] = s.all_tx[...]

    def all_copy(p, source):
        return send(s.all_tx, s.all_rx.at[source], s.all_sem, p, source, dp=p)

    others(n_dp, image, lambda p: all_copy(p, image).start())
    others(n_dp, image, lambda p: all_copy(p, p).wait_recv())
    s.last_tx[...] = slots(s.all_rx, n_dp).astype(BF16)
    s.last_rx[me] = s.last_tx[...]

    def last_copy(p, source):
        return send(s.last_tx, s.last_rx.at[source], s.last_sem, p, source, sp=p)

    others(n_sp, me, lambda p: last_copy(p, me).start())

    others(n_dp, image, lambda p: q_copy(p, p).wait_recv())
    others(n_dp, image, lambda p: side_copy(p, p).wait_recv())
    here = s.emb[:, pl.ds(pl.multiple_of(image * block, block), block)].astype(F32) - mean_col
    here_t = here.T
    s.emb_t[...] = here_t
    which = lax.broadcasted_iota(jnp.int32, (n_dp, block), 0)
    shifts = jnp.zeros((n_dp, block), F32)
    sums = jnp.zeros((n_dp, block), F32)
    for k in range(n_dp):
        shifts = jnp.where(which == k, s.side_rx[k, 1:2, :], shifts)
        sums = jnp.where(which == k, s.side_rx[k, 2:3, :], sums)
    out_up[...] = exact(shifts, sums, ((0,), (0,)))

    def up_part(k):
        left = here_t * s.side_rx[k].T[:, 0:1]
        out_up[...] += nn(left.astype(BF16), s.q_rx[k])

    for k in range(n_dp):
        up_part(k)

    others(n_sp, me, lambda p: last_copy(p, p).wait_recv())

    def show(k):
        out_conv[rows_at(k), :] = s.last_rx[k].astype(F32)

    every(n_sp, show)

    for copy in (mix_copy, off_copy, pair_copy, sum_copy):
        copy.wait_send()

    def left(p):
        for copy in (stat_copy(p), act_copy(p, me), part_copy(p, me), stat2_copy(p, me), grad_copy(p, me)):
            copy.wait_send()
        last_copy(p, me).wait_send()

    others(n_sp, me, left)

    def left_dp(p):
        for copy in (down_out(p, image, p), q_copy(p, image), side_copy(p, image), all_copy(p, image)):
            copy.wait_send()

    others(n_dp, image, left_dp)

    def left_block(p):
        sib_copy(p).wait_send()
        for name in routes:
            cot_copy(name, p).wait_send()

    every(n_dp, left_block)


class Scratch:
    def __init__(self, names, refs):
        for name, ref in zip(names, refs):
            setattr(self, name, ref)


def on_device(
    n_sp, n_dp, feats, conv_w, group_norm_gain, group_norm_bias, emb_w, time_w, up_w, down_w, steps, cotangent
):
    image = feats[0]
    rows_in, cols_in, in_chans = image.shape
    rows, cols = rows_in // 2, cols_in // 2
    rim = lax.ppermute(image[:, cols_in - 1, :], "sp", [(i, i + 1) for i in range(n_sp - 1)])
    widened = jnp.concatenate([rim[:, None, :], image], axis=1)
    padded = jnp.pad(widened, ((1, 0), (0, 0), (0, 0)))
    pieces = []
    for row_tap in range(3):
        for col_tap in range(3):
            pieces.append(padded[row_tap : row_tap + 2 * rows : 2, col_tap : col_tap + 2 * cols : 2, :])
    pixels = rows * cols
    patches = jnp.concatenate(pieces, axis=-1).reshape(pixels, 9 * in_chans)
    freq_count = time_w.shape[0] // 2
    freqs = jnp.exp(-math.log(10000.0) * jnp.arange(freq_count, dtype=F32) / freq_count)
    angle = steps[0].astype(F32) * freqs
    embed = jax.nn.silu(jnp.concatenate([jnp.cos(angle), jnp.sin(angle)])).astype(BF16)
    es = jnp.broadcast_to(embed[None, :], (16, embed.shape[0]))
    gain_bias = jnp.concatenate(
        [group_norm_gain[None], group_norm_bias[None], jnp.zeros((6, group_norm_gain.shape[0]), F32)]
    )
    chans = conv_w.shape[1]
    width = emb_w.shape[1]
    hidden = up_w.shape[1]
    block = width // n_dp
    n_chip = n_sp // 2
    taps = conv_w.shape[0] // n_sp
    half = pixels // 2
    tokens = n_chip * pixels
    vm = pltpu.VMEM
    dma = lambda n: pltpu.SemaphoreType.DMA((2, n))
    scratch = dict(
        load=pltpu.SemaphoreType.DMA((8 + 2 * n_dp,)),
        stat_sem=dma(n_sp), act_sem=dma(n_sp), part_sem=dma(n_sp), stat2_sem=dma(n_sp),
        grad_sem=dma(n_sp), last_sem=dma(n_sp), cot_sem=dma(9 * n_dp), pair_sem=dma(8),
        sib_sem=dma(n_dp), gd_sem=dma(n_dp), q_sem=dma(n_dp), side_sem=dma(n_dp), all_sem=dma(n_dp),
        patches=vm(patches.shape, BF16), conv=vm(conv_w.shape, BF16), emb=vm(emb_w.shape, BF16),
        time=vm((2, time_w.shape[0], 1024), BF16), up=vm(up_w.shape, BF16),
        gated=vm((n_dp, 2 * hidden, block), BF16), cot=vm((n_dp, n_chip, pixels, block), BF16),
        z=vm((pixels, chans), F32), slope0=vm((pixels, chans), F32), rstd=vm((8, chans), F32),
        stat_tx=vm((8, chans), F32), stat_rx=vm((n_sp, 8, chans), F32),
        stat2_tx=vm((8, chans), F32), stat2_rx=vm((n_sp, 8, chans), F32),
        mod=vm((16, 3 * width), F32), act_tx=vm((2, half, chans), BF16),
        act_rx=vm((n_sp, half, chans), BF16), act=vm((n_chip, pixels, chans), F32),
        act_t=vm((chans, tokens), BF16), mean_col=vm((chans, 128), F32), gram=vm((chans, chans), F32),
        gram_hi=vm((chans, chans), BF16), gram_lo=vm((chans, chans), BF16),
        mix=vm((chans, hidden), F32), mixer=vm((chans, 2 * hidden), BF16),
        offset=vm((16, hidden), F32), offsets=vm((16, 2 * hidden), F32), skip=vm((pixels, chans), F32),
        hid_t=vm((2 * hidden, tokens), BF16), slope=vm((n_chip, pixels, 2 * hidden), F32),
        moved=vm((n_chip, pixels, 2 * hidden), F32), dhid=vm((n_chip, pixels, 2 * hidden), F32),
        spread=vm((n_chip, pixels, chans), F32), token_rstd=vm((n_chip, pixels, 128), F32),
        patches_t=vm((patches.shape[1], pixels), BF16),
        sib_tx=vm((n_dp, hidden, block), BF16), sib_rx=vm((n_dp, hidden, block), BF16),
        gd_own=vm((2, hidden, block), F32), gd_tx=vm((n_dp, hidden, block), BF16),
        gd_rx=vm((n_dp, hidden, block), BF16), du_sum=vm((8, 2 * hidden), F32),
        du=vm((tokens, 2 * hidden), BF16), part_tx=vm((n_sp, half, chans), BF16),
        part_rx=vm((n_sp, half, chans), BF16), pairs=vm((chans, 2 * hidden), F32),
        pair_tx=vm((chans, hidden), BF16), pair_rx=vm((chans, hidden), BF16),
        sum_tx=vm((8, hidden), F32), sum_rx=vm((8, hidden), F32), q_tx=vm((chans, hidden), BF16),
        q_rx=vm((n_dp, chans, hidden), BF16), side_tx=vm((n_dp, 8, block), F32),
        side_rx=vm((n_dp, 8, block), F32), grad=vm((conv_w.shape[0], chans), F32),
        grad_tx=vm((n_sp, taps, chans), BF16), grad_rx=vm((n_sp, taps, chans), BF16),
        all_tx=vm((taps, chans), BF16), all_rx=vm((n_dp, taps, chans), BF16),
        last_tx=vm((taps, chans), BF16), last_rx=vm((n_sp, taps, chans), BF16),
        emb_t=vm((block, chans), F32),
    )
    names = tuple(scratch)

    def kernel(*refs):
        body(n_sp, n_dp, *refs[:12], Scratch(names, refs[12:]))

    in_vmem = pl.BlockSpec(memory_space=pltpu.VMEM)
    in_place = pl.BlockSpec(memory_space=pl.ANY)
    return pl.pallas_call(
        kernel,
        out_shape=(
            jax.ShapeDtypeStruct(conv_w.shape, F32),
            jax.ShapeDtypeStruct((block, hidden), F32),
            jax.ShapeDtypeStruct((hidden, block), F32),
        ),
        in_specs=[in_vmem] * 2 + [in_place] * 7,
        out_specs=(in_vmem,) * 3,
        scratch_shapes=list(scratch.values()),
        compiler_params=pltpu.CompilerParams(
            collective_id=0, has_side_effects=True, vmem_limit_bytes=67043328
        ),
    )(es, gain_bias, patches, conv_w, emb_w, time_w, up_w, down_w, cotangent[0])


def solution(mesh):
    in_specs = (
        P("dp", None, "sp", None),
        P(),
        P(),
        P(),
        P(),
        P(),
        P(None, "sp"),
        P("sp", None),
        P("dp"),
        P("dp", "sp", None),
    )
    out_specs = (P(), P("dp", "sp"), P("sp", "dp"))
    return jax.shard_map(
        functools.partial(on_device, mesh.shape["sp"], mesh.shape["dp"]),
        mesh=mesh,
        in_specs=in_specs,
        out_specs=out_specs,
        check_vma=False,
    )
```

time: 590 us -> 181 us (0.31)
  waiting for transfers between devices: 422 us -> 0.01 us
  Pallas kernels: 0 us -> 162 us
  matrix products: 63.3 us -> 0 us
  blocking collectives: 22.2 us -> 0 us
  local copies, waits for them, and re-layouts: 29.3 us -> 8.91 us
  other arithmetic: 17.9 us -> 1.48 us
  between operations: 14.8 us -> 1.47 us
  starting transfers between devices: 19.6 us -> 6.89 us
    pallas_call x0 -> x1, Pallas kernels: none -> 162 us  [on_device(): pl.pallas_call(kernel, out_shape=(jax.ShapeDtypeStruct(conv_w.shape, F32)...]
    psum x1 -> x0, waiting for transfers between devices: 155 us -> none  [on_device(): grad_conv = lax.psum(conv_local, DP_SP)]
    all_gather x1 -> x0, waiting for transfers between devices: 147 us -> none  [side_by_side(): lax.all_gather(both, axis, axis=dim, tiled=True)]
    reduce_scatter x3 -> x0, waiting for transfers between devices: 109 us -> none  [the longest x1 79.5 us: sum_by_chip(): return lax.psum_scatter(parts, chips, scatter_dimension=0, tiled=True)[0]]
    dot_general x10 -> x0, matrix products: 63.3 us -> none  [the longest x6 47.3 us: contract(): lax.dot_general(left, right, (((left_dim,), (right_dim,)), ((), ())), pre...]
    all_to_all x2 -> x0, blocking collectives: 22.2 us -> none  [the longest x1 12.2 us: on_device(): lax.all_to_all(dact.reshape(seq_rows, cols * devices_sp, channel_count).a...]
    all_to_all x2 -> x0, starting transfers between devices: 11.9 us -> none  [the longest x1 7.93 us: copy_for_each(): lax.all_to_all(jnp.broadcast_to(array[None], (length, *array.shape)), axi...]
    all_to_all x2 -> x0, waiting for transfers between devices: 11.2 us -> none  [the longest x1 7.37 us: on_device(): lax.all_to_all(act_b.reshape(rows, cols, channel_count), SP, split_axis=0...]
  transfers between devices with their start and end apart: 8 -> 1, of which waited for: 6 -> 0; matrix products, arithmetic and copies ran while one was open for 10% -> 1% of each run, Pallas kernels for 0% -> 0%
where the time goes in v2:
time: 181 us
  Pallas kernels  162 us (90%)
  local copies, waits for them, and re-layouts  8.91 us (5%)
  starting transfers between devices  6.89 us (4%)
    pallas_call x1, Pallas kernels, on_device(): pl.pallas_call(kernel, out_shape=(jax.ShapeDtypeStruct(conv_w.shape, F32)...  162 us
    ppermute x1, starting transfers between devices, on_device(): lax.ppermute(image[:, cols_in - 1, :], 'sp', [(i, i + 1) for i in range(n...  6.89 us
    unnamed x16, local copies, waits for them, and re-layouts  5.13 us
  transfers between devices with their start and end apart: 1, of which 0 were waited for; matrix products, arithmetic and copies ran while one was open for 1% of the time, Pallas kernels for 0%

profile of v2, /device:TPU:1, one launch (start us, length us, event | category | flops | bytes accessed | tf_op | source)
XLA Modules:
  0.0 180.8 jit_solution(6827226023775938138)
XLA Ops:
  0.6 0.9 copy.19
  1.6 6.9 %collective-permute-start = (bf16[32,128]{1,0:T(8,128)(2,1)S(1)}, bf16[32,128]{1,0:T(8,128)(2,1)S(1)}, u32[]{:S(2)}, u32[]{:S(2)}) collective-permute-start(bf16[32,128]{1,0:T(8,128)(2,1)S(1)} %slice_bitcast_fusion), channel_id=1, source_target_pairs={{0,1},{1,2},{2,3},{3,4},{4,5},{5,6},{6,7},{7,8},{8,9},{9,10},{10,1... | collective-permute-start | bytes 24584 | tf_op jit(solution)/shard_map/ppermute | solution.py:585
  9.2 0.1 pad.9.clone
  9.3 1.4 maximum_maximum_fusion.refs_1_
  10.6 0.0 collective-permute-done
  10.7 0.1 fusion.2
  10.7 0.2 slice.38
  10.9 0.2 slice.37
  11.2 0.3 slice.36
  11.5 0.2 slice.35
  11.7 0.2 slice.34
  11.9 0.3 slice.33
  12.3 0.2 slice.32
  12.5 0.2 slice.31
  12.7 0.4 slice.39
  13.3 0.8 copy.18
  14.0 0.6 broadcast_in_dim.18.refs_0_
  14.6 162.1 %shard_map.121 = (f32[1152,256]{1,0:T(8,128)}, f32[384,384]{1,0:T(8,128)}, f32[384,384]{1,0:T(8,128)}) custom-call(bf16[16,256]{1,0:T(8,128)(2,1)} %broadcast_in_dim.18.refs_0_, f32[8,256]{1,0:T(8,128)} %maximum_maximum_fusion.refs_1_, bf16[128,1152]{1,0:T(8,128)(2,1)} %bitcast.13, bf16[1152,256]{1,0:T(8,128)(2,1)} %refs_3_.1, bf16[256,3072]{1,0:T(8,128)(2,1)} %refs_4_.1, ...), custom_call_target="tpu_custom_call" | custom-call | tf_op jit(solution)/shard_map/pallas_call | solution.py:654
  176.7 0.0 copy-start.1
  176.7 0.0 copy-start
  176.7 2.5 %copy.32 = f32[1152,256]{1,0:T(8,128)} copy(f32[1152,256]{1,0:T(8,128)} %get-tuple-element.8) | data formatting | bytes 2359296
  179.2 0.0 copy-done.1
  179.2 0.8 copy.33
  180.0 0.0 copy-done
  180.0 0.8 copy.34
  (13 shorter events, 0.2 us)
Async XLA Ops:
  1.6 9.1 %collective-permute-start = (bf16[32,128]{1,0:T(8,128)(2,1)S(1)}, bf16[32,128]{1,0:T(8,128)(2,1)S(1)}, u32[]{:S(2)}, u32[]{:S(2)}) collective-permute-start(bf16[32,128]{1,0:T(8,128)(2,1)S(1)} %slice_bitcast_fusion), channel_id=1, source_target_pairs={{0,1},{1,2},{2,3},{3,4},{4,5},{5,6},{6,7},{7,8},{8,9},{9,10},{10,1... | collective-permute-start | bytes 24584 | tf_op jit(solution)/shard_map/ppermute | solution.py:585
  176.7 2.5 %copy-start.1 = (f32[384,384]{1,0:T(8,128)S(1)}, f32[384,384]{1,0:T(8,128)}, u32[]{:S(2)}) copy-start(f32[384,384]{1,0:T(8,128)} %get-tuple-element.9) | copy-start | bytes 1769476
  176.7 3.3 %copy-start = (f32[384,384]{1,0:T(8,128)S(1)}, f32[384,384]{1,0:T(8,128)}, u32[]{:S(2)}) copy-start(f32[384,384]{1,0:T(8,128)} %get-tuple-element.10) | copy-start | bytes 1769476

commit v3 on v2

--- a/solution.py
+++ b/solution.py
@@ -54,7 +54,7 @@
 
 
 def body(
-    n_sp, n_dp, es, gain_bias, patches_in, conv_in, emb_in, time_in, up_in, down_in, cot_in,
+    n_sp, n_dp, es, gain, bias, planes, conv_in, emb_in, time_in, up_in, down_in, cot_in,
     out_conv, out_up, out_down, s,
 ):
     n_chip = n_sp // 2
@@ -62,7 +62,8 @@
     hidden = up_in.shape[1]
     block = width // n_dp
     chans = conv_in.shape[1]
-    pixels = patches_in.shape[0]
+    rows, cols, in_chans = planes.shape[2:]
+    pixels = rows * cols
     half = pixels // 2
     taps = conv_in.shape[0] // n_sp
     me = lax.axis_index("sp")
@@ -104,7 +105,6 @@
     loads = {}
     for index, (name, src, dst) in enumerate(
         (
-            ("patches", patches_in, s.patches),
             ("conv", conv_in, s.conv),
             ("emb", emb_in, s.emb),
             ("up", up_in, s.up),
@@ -127,27 +127,61 @@
 
     def time_load(k):
         columns = pl.ds(pl.multiple_of(k * 1024, 1024), 1024)
-        slot = lax.rem(k, 2)
-        return pltpu.make_async_copy(time_in.at[:, columns], s.time.at[slot], s.load.at[6 + slot])
-
-    loads["patches"].start()
+        return pltpu.make_async_copy(time_in.at[:, columns], s.time.at[k], s.load.at[8 + 2 * n_dp + k])
+
+    n_time = 3 * width // 1024
+
     loads["conv"].start()
     every(n_dp, lambda p: cot_load(p).start())
     every(n_dp, lambda p: down_load(p).start())
-    time_load(0).start()
+    every(n_time, lambda k: time_load(k).start())
     for name in ("emb", "up"):
         loads[name].start()
 
-    loads["patches"].wait()
+    for parity in range(2):
+        s.rim_tx[parity] = planes[parity, 1].astype(F32)[:, cols - 1, :].astype(BF16)
+
+    @pl.when(me == 0)
+    def _():
+        s.rim_rx[...] = jnp.zeros_like(s.rim_rx)
+
+    pl.semaphore_wait(barrier, n_sp - 1 + n_dp - 1)
+    rim_copy = send(s.rim_tx, s.rim_rx, s.pair_sem, 5, 5, sp=lax.rem(me + 1, n_sp))
+
+    @pl.when(me < n_sp - 1)
+    def _():
+        rim_copy.start()
+
+    first_column = lax.broadcasted_iota(jnp.int32, (rows, cols, in_chans), 1) == 0
+
+    def patch(row_tap, col_tap):
+        parity = (row_tap + 1) % 2
+        value = planes[parity, (col_tap + 1) % 2].astype(F32)
+        if col_tap == 0:
+            value = pltpu.roll(value, 1, 1)
+            value = jnp.where(first_column, s.rim_rx[parity].astype(F32)[:, None, :], value)
+        if row_tap == 0:
+            value = jnp.concatenate([jnp.zeros_like(value[:1]), value[:-1]], axis=0)
+        tap = row_tap * 3 + col_tap
+        s.patches[:, tap * in_chans : (tap + 1) * in_chans] = value.reshape(pixels, in_chans).astype(BF16)
+
+    for row_tap in range(3):
+        for col_tap in (1, 2):
+            patch(row_tap, col_tap)
     loads["conv"].wait()
+
+    @pl.when(me > 0)
+    def _():
+        rim_copy.wait_recv()
+
+    for row_tap in range(3):
+        patch(row_tap, 0)
     s.z[...] = nn(s.patches[...], s.conv[...])
     z = s.z[...]
     s.stat_tx[...] = rows_of(
         jnp.sum(z, axis=0, keepdims=True), jnp.sum(z * z, axis=0, keepdims=True), (8, chans)
     )
     s.stat_rx[me] = s.stat_tx[...]
-
-    pl.semaphore_wait(barrier, n_sp - 1 + n_dp - 1)
 
     def stat_copy(p):
         return send(s.stat_tx, s.stat_rx.at[me], s.stat_sem, p, me, sp=p)
@@ -188,18 +222,18 @@
         for name in ("z", "e", "w"):
             cot_copy(name, p).start()
 
-    def relay(q):
+    def relay(q, steps):
         p = turn(q)
-        for name, then in (
-            ("z", ("ez", "wz")),
-            ("e", ("ee",)),
-            ("w", ("ww",)),
-            ("ez", ("eez",)),
-            ("wz", ("wwz",)),
-        ):
+        for name, then in steps:
             cot_copy(name, p, True).wait_recv()
             for onward in then:
                 cot_copy(onward, p).start()
+
+    def relay_near(q):
+        relay(q, (("z", ("ez", "wz")), ("e", ("ee",)), ("w", ("ww",))))
+
+    def relay_far(q):
+        relay(q, (("ez", ("eez",)), ("wz", ("wwz",))))
 
     def landed(q):
         p = turn(q)
@@ -214,16 +248,10 @@
     down_copy = send(my_down, my_down, s.pair_sem, 0, 0, sp=sibling)
     down_copy.start()
 
-    n_time = 3 * width // 1024
-
     def mod_part(k):
-        @pl.when(k + 1 < n_time)
-        def _():
-            time_load(k + 1).start()
-
         columns = pl.ds(pl.multiple_of(k * 1024, 1024), 1024)
         time_load(k).wait()
-        s.mod[:, columns] = nn(es[...], s.time[lax.rem(k, 2)])
+        s.mod[:, columns] = nn(es[...], s.time[k])
 
     every(n_time, mod_part)
 
@@ -243,9 +271,9 @@
     s.rstd[...] = jnp.broadcast_to(rstd, s.rstd.shape)
     xhat = (s.z[...] - mean) * rstd
     s.z[...] = xhat
-    pre = xhat * gain_bias[0:1, :] + gain_bias[1:2, :]
+    pre = xhat * gain[...] + bias[...]
     sigma = jax.nn.sigmoid(pre)
-    s.slope0[...] = sigma * (1.0 + pre * (1.0 - sigma)) * gain_bias[0:1, :]
+    s.slope0[...] = sigma * (1.0 + pre * (1.0 - sigma)) * gain[...]
     act = (pre * sigma).reshape(n_chip, 2, pixels // n_sp, chans)
     for k in range(2):
         s.act_tx[k] = act[:, k].reshape(half, chans).astype(BF16)
@@ -256,7 +284,8 @@
 
     others(n_sp, me, lambda p: act_copy(p, me).start())
     own(2)
-    relay(0)
+    relay_near(0)
+    own(3)
 
     loads["emb"].wait()
     loads["up"].wait()
@@ -291,8 +320,9 @@
     mix_copy.start()
     off_copy = send(s.offsets.at[:, my_cols], s.offsets.at[:, my_cols], s.pair_sem, 2, 2, sp=sibling)
     off_copy.start()
-    own(3)
-    relay(1)
+    relay_near(1)
+    relay_far(0)
+    own(4)
 
     down_from = send(its_down, its_down, s.pair_sem, 0, 0, sp=sibling)
     down_copy.wait_send()
@@ -336,6 +366,8 @@
         s.token_rstd[i] = jnp.broadcast_to(token_rstd, (pixels, 128))
         s.dhid[i] = jnp.zeros_like(slope)
 
+    relay_near(2)
+    relay_far(1)
     every(n_chip, forward)
     s.patches_t[...] = s.patches[...].astype(F32).T.astype(BF16)
 
@@ -372,13 +404,17 @@
 
     @pl.loop(0, n_dp)
     def _(q):
-        @pl.when(q + 4 < n_dp)
+        @pl.when(q + 5 < n_dp)
         def _():
-            own(q + 4)
+            own(q + 5)
+
+        @pl.when(q + 3 < n_dp)
+        def _():
+            relay_near(q + 3)
 
         @pl.when(q + 2 < n_dp)
         def _():
-            relay(q + 2)
+            relay_far(q + 2)
 
         @pl.when(q > 0)
         def _():
@@ -424,6 +460,44 @@
     sum_copy.start()
     _, total = whole(n_dp - 1)
     out_down[...] = total
+
+    pair_copy.wait_recv()
+    sum_copy.wait_recv()
+    s.q_tx[...] = (s.pairs[:, my_cols] + s.pair_rx[...].astype(F32)).astype(BF16)
+    s.q_rx[image] = s.q_tx[...]
+    du_sum = (s.du_sum[:, my_cols] + s.sum_rx[...])[0:1, :]
+
+    def side_of(p):
+        shift = s.mod[0:1, pl.ds(pl.multiple_of(p * block, block), block)]
+        scale = s.mod[0:1, pl.ds(pl.multiple_of(width + p * block, block), block)]
+        which = lax.broadcasted_iota(jnp.int32, (8, block), 0)
+        return jnp.where(which == 2, du_sum, rows_of(1.0 + scale, shift, (8, block)))
+
+    def q_copy(p, source):
+        return send(s.q_tx, s.q_rx.at[source], s.q_sem, p, source, dp=p)
+
+    def side_copy(p, source):
+        return send(s.side_tx.at[p], s.side_rx.at[source], s.side_sem, p, source, dp=p)
+
+    n_row = n_dp // 2
+    row_first = image // n_row * n_row
+    twin = lax.rem(image + n_row, n_dp)
+
+    def in_row(act):
+        others(n_row, image - row_first, lambda at: act(row_first + at))
+
+    def forward_copy(p):
+        at = lax.rem(p + n_row, n_dp)
+        return send(s.q_rx.at[twin], s.q_rx.at[twin], s.q_sem, at, twin, dp=p)
+
+    def side_out(p):
+        s.side_tx[p] = side_of(p)
+        side_copy(p, image).start()
+
+    q_copy(twin, image).start()
+    in_row(lambda p: q_copy(p, image).start())
+    others(n_dp, image, side_out)
+    s.side_rx[image] = side_of(image)
 
     others(n_sp, me, lambda p: part_copy(p, p).wait_recv())
     parts = []
@@ -444,32 +518,6 @@
 
     others(n_sp, me, lambda p: stat2_copy(p, me).start())
 
-    pair_copy.wait_recv()
-    sum_copy.wait_recv()
-    s.q_tx[...] = (s.pairs[:, my_cols] + s.pair_rx[...].astype(F32)).astype(BF16)
-    s.q_rx[image] = s.q_tx[...]
-    du_sum = (s.du_sum[:, my_cols] + s.sum_rx[...])[0:1, :]
-
-    def side_of(p):
-        shift = s.mod[0:1, pl.ds(pl.multiple_of(p * block, block), block)]
-        scale = s.mod[0:1, pl.ds(pl.multiple_of(width + p * block, block), block)]
-        which = lax.broadcasted_iota(jnp.int32, (8, block), 0)
-        return jnp.where(which == 2, du_sum, rows_of(1.0 + scale, shift, (8, block)))
-
-    def q_copy(p, source):
-        return send(s.q_tx, s.q_rx.at[source], s.q_sem, p, source, dp=p)
-
-    def side_copy(p, source):
-        return send(s.side_tx.at[p], s.side_rx.at[source], s.side_sem, p, source, dp=p)
-
-    def q_out(p):
-        q_copy(p, image).start()
-        s.side_tx[p] = side_of(p)
-        side_copy(p, image).start()
-
-    others(n_dp, image, q_out)
-    s.side_rx[image] = side_of(image)
-
     others(n_sp, me, lambda p: stat2_copy(p, p).wait_recv())
     first, second = group_sums(s.stat2_rx)
     dz = (s.rstd[0:1, :] * (s.slope0[...] - first - s.z[...] * second)).astype(BF16)
@@ -478,15 +526,50 @@
     def rows_at(k):
         return pl.ds(pl.multiple_of(k * taps, 8), taps)
 
-    def grad_copy(p, source):
-        return send(s.grad_tx.at[p], s.grad_rx.at[source], s.grad_sem, p, source, sp=p)
-
-    def grad_out(p):
-        s.grad_tx[p] = s.grad[rows_at(p), :].astype(BF16)
-        grad_copy(p, me).start()
-
-    others(n_sp, me, grad_out)
-    s.grad_rx[me] = s.grad[rows_at(me), :].astype(BF16)
+    n_half = 2
+    lanes_of = lambda h: slice(h * (chans // n_half), (h + 1) * (chans // n_half))
+
+    def grad_copy(h, p, source):
+        at = h * n_sp
+        return send(s.grad_tx.at[h, p], s.grad_rx.at[h, source], s.grad_sem, at + p, at + source, sp=p)
+
+    def all_copy(h, p, source):
+        at = h * n_dp
+        return send(s.all_tx.at[h], s.all_rx.at[h, source], s.all_sem, at + p, at + source, dp=p)
+
+    def last_copy(h, p, source):
+        at = h * n_sp
+        return send(s.last_tx.at[h], s.last_rx.at[h, source], s.last_sem, at + p, at + source, sp=p)
+
+    for h in range(n_half):
+
+        def grad_out(p, h=h):
+            s.grad_tx[h, p] = s.grad[rows_at(p), lanes_of(h)].astype(BF16)
+            grad_copy(h, p, me).start()
+
+        others(n_sp, me, grad_out)
+        s.grad_rx[h, me] = s.grad[rows_at(me), lanes_of(h)].astype(BF16)
+
+    def slots(ref, h, n):
+        total = ref[h, 0].astype(F32)
+        for j in range(1, n):
+            total = total + ref[h, j].astype(F32)
+        return total
+
+    for h in range(n_half):
+        others(n_sp, me, lambda p: grad_copy(h, p, p).wait_recv())
+        s.all_tx[h] = slots(s.grad_rx, h, n_sp).astype(BF16)
+        s.all_rx[h, image] = s.all_tx[h]
+        others(n_dp, image, lambda p: all_copy(h, p, image).start())
+
+    q_copy(twin, twin).wait_recv()
+    in_row(lambda p: forward_copy(p).start())
+
+    for h in range(n_half):
+        others(n_dp, image, lambda p: all_copy(h, p, p).wait_recv())
+        s.last_tx[h] = slots(s.all_rx, h, n_dp).astype(BF16)
+        s.last_rx[h, me] = s.last_tx[h]
+        others(n_sp, me, lambda p: last_copy(h, p, me).start())
 
     others(n_dp, image, lambda p: down_out(p, p, p).wait_recv())
 
@@ -495,31 +578,8 @@
 
     others(n_dp, image, add_down)
 
-    others(n_sp, me, lambda p: grad_copy(p, p).wait_recv())
-
-    def slots(ref, n):
-        total = ref[0].astype(F32)
-        for j in range(1, n):
-            total = total + ref[j].astype(F32)
-        return total
-
-    s.all_tx[...] = slots(s.grad_rx, n_sp).astype(BF16)
-    s.all_rx[image] = s.all_tx[...]
-
-    def all_copy(p, source):
-        return send(s.all_tx, s.all_rx.at[source], s.all_sem, p, source, dp=p)
-
-    others(n_dp, image, lambda p: all_copy(p, image).start())
-    others(n_dp, image, lambda p: all_copy(p, p).wait_recv())
-    s.last_tx[...] = slots(s.all_rx, n_dp).astype(BF16)
-    s.last_rx[me] = s.last_tx[...]
-
-    def last_copy(p, source):
-        return send(s.last_tx, s.last_rx.at[source], s.last_sem, p, source, sp=p)
-
-    others(n_sp, me, lambda p: last_copy(p, me).start())
-
-    others(n_dp, image, lambda p: q_copy(p, p).wait_recv())
+    in_row(lambda p: q_copy(p, p).wait_recv())
+    in_row(lambda p: q_copy(p, lax.rem(p + n_row, n_dp)).wait_recv())
     others(n_dp, image, lambda p: side_copy(p, p).wait_recv())
     here = s.emb[:, pl.ds(pl.multiple_of(image * block, block), block)].astype(F32) - mean_col
     here_t = here.T
@@ -539,26 +599,35 @@
     for k in range(n_dp):
         up_part(k)
 
-    others(n_sp, me, lambda p: last_copy(p, p).wait_recv())
-
-    def show(k):
-        out_conv[rows_at(k), :] = s.last_rx[k].astype(F32)
-
-    every(n_sp, show)
+    for h in range(n_half):
+        others(n_sp, me, lambda p: last_copy(h, p, p).wait_recv())
+
+        def show(k, h=h):
+            out_conv[rows_at(k), lanes_of(h)] = s.last_rx[h, k].astype(F32)
+
+        every(n_sp, show)
 
     for copy in (mix_copy, off_copy, pair_copy, sum_copy):
         copy.wait_send()
 
+    @pl.when(me < n_sp - 1)
+    def _():
+        rim_copy.wait_send()
+
     def left(p):
-        for copy in (stat_copy(p), act_copy(p, me), part_copy(p, me), stat2_copy(p, me), grad_copy(p, me)):
+        for copy in (stat_copy(p), act_copy(p, me), part_copy(p, me), stat2_copy(p, me)):
             copy.wait_send()
-        last_copy(p, me).wait_send()
+        for h in range(n_half):
+            grad_copy(h, p, me).wait_send()
+            last_copy(h, p, me).wait_send()
 
     others(n_sp, me, left)
 
     def left_dp(p):
-        for copy in (down_out(p, image, p), q_copy(p, image), side_copy(p, image), all_copy(p, image)):
+        for copy in (down_out(p, image, p), q_copy(p, image), side_copy(p, image)):
             copy.wait_send()
+        for h in range(n_half):
+            all_copy(h, p, image).wait_send()
 
     others(n_dp, image, left_dp)
 
@@ -582,23 +651,13 @@
     image = feats[0]
     rows_in, cols_in, in_chans = image.shape
     rows, cols = rows_in // 2, cols_in // 2
-    rim = lax.ppermute(image[:, cols_in - 1, :], "sp", [(i, i + 1) for i in range(n_sp - 1)])
-    widened = jnp.concatenate([rim[:, None, :], image], axis=1)
-    padded = jnp.pad(widened, ((1, 0), (0, 0), (0, 0)))
-    pieces = []
-    for row_tap in range(3):
-        for col_tap in range(3):
-            pieces.append(padded[row_tap : row_tap + 2 * rows : 2, col_tap : col_tap + 2 * cols : 2, :])
     pixels = rows * cols
-    patches = jnp.concatenate(pieces, axis=-1).reshape(pixels, 9 * in_chans)
+    planes = image.reshape(rows, 2, cols, 2, in_chans).transpose(1, 3, 0, 2, 4)
     freq_count = time_w.shape[0] // 2
     freqs = jnp.exp(-math.log(10000.0) * jnp.arange(freq_count, dtype=F32) / freq_count)
     angle = steps[0].astype(F32) * freqs
     embed = jax.nn.silu(jnp.concatenate([jnp.cos(angle), jnp.sin(angle)])).astype(BF16)
     es = jnp.broadcast_to(embed[None, :], (16, embed.shape[0]))
-    gain_bias = jnp.concatenate(
-        [group_norm_gain[None], group_norm_bias[None], jnp.zeros((6, group_norm_gain.shape[0]), F32)]
-    )
     chans = conv_w.shape[1]
     width = emb_w.shape[1]
     hidden = up_w.shape[1]
@@ -610,12 +669,13 @@
     vm = pltpu.VMEM
     dma = lambda n: pltpu.SemaphoreType.DMA((2, n))
     scratch = dict(
-        load=pltpu.SemaphoreType.DMA((8 + 2 * n_dp,)),
+        load=pltpu.SemaphoreType.DMA((8 + 2 * n_dp + time_w.shape[1] // 1024,)),
         stat_sem=dma(n_sp), act_sem=dma(n_sp), part_sem=dma(n_sp), stat2_sem=dma(n_sp),
-        grad_sem=dma(n_sp), last_sem=dma(n_sp), cot_sem=dma(9 * n_dp), pair_sem=dma(8),
-        sib_sem=dma(n_dp), gd_sem=dma(n_dp), q_sem=dma(n_dp), side_sem=dma(n_dp), all_sem=dma(n_dp),
-        patches=vm(patches.shape, BF16), conv=vm(conv_w.shape, BF16), emb=vm(emb_w.shape, BF16),
-        time=vm((2, time_w.shape[0], 1024), BF16), up=vm(up_w.shape, BF16),
+        grad_sem=dma(2 * n_sp), last_sem=dma(2 * n_sp), cot_sem=dma(9 * n_dp), pair_sem=dma(8),
+        sib_sem=dma(n_dp), gd_sem=dma(n_dp), q_sem=dma(n_dp), side_sem=dma(n_dp), all_sem=dma(2 * n_dp),
+        patches=vm((pixels, 9 * in_chans), BF16), rim_tx=vm((2, rows, in_chans), BF16),
+        rim_rx=vm((2, rows, in_chans), BF16), conv=vm(conv_w.shape, BF16), emb=vm(emb_w.shape, BF16),
+        time=vm((time_w.shape[1] // 1024, time_w.shape[0], 1024), BF16), up=vm(up_w.shape, BF16),
         gated=vm((n_dp, 2 * hidden, block), BF16), cot=vm((n_dp, n_chip, pixels, block), BF16),
         z=vm((pixels, chans), F32), slope0=vm((pixels, chans), F32), rstd=vm((8, chans), F32),
         stat_tx=vm((8, chans), F32), stat_rx=vm((n_sp, 8, chans), F32),
@@ -629,7 +689,7 @@
         hid_t=vm((2 * hidden, tokens), BF16), slope=vm((n_chip, pixels, 2 * hidden), F32),
         moved=vm((n_chip, pixels, 2 * hidden), F32), dhid=vm((n_chip, pixels, 2 * hidden), F32),
         spread=vm((n_chip, pixels, chans), F32), token_rstd=vm((n_chip, pixels, 128), F32),
-        patches_t=vm((patches.shape[1], pixels), BF16),
+        patches_t=vm((9 * in_chans, pixels), BF16),
         sib_tx=vm((n_dp, hidden, block), BF16), sib_rx=vm((n_dp, hidden, block), BF16),
         gd_own=vm((2, hidden, block), F32), gd_tx=vm((n_dp, hidden, block), BF16),
         gd_rx=vm((n_dp, hidden, block), BF16), du_sum=vm((8, 2 * hidden), F32),
@@ -639,15 +699,15 @@
         sum_tx=vm((8, hidden), F32), sum_rx=vm((8, hidden), F32), q_tx=vm((chans, hidden), BF16),
         q_rx=vm((n_dp, chans, hidden), BF16), side_tx=vm((n_dp, 8, block), F32),
         side_rx=vm((n_dp, 8, block), F32), grad=vm((conv_w.shape[0], chans), F32),
-        grad_tx=vm((n_sp, taps, chans), BF16), grad_rx=vm((n_sp, taps, chans), BF16),
-        all_tx=vm((taps, chans), BF16), all_rx=vm((n_dp, taps, chans), BF16),
-        last_tx=vm((taps, chans), BF16), last_rx=vm((n_sp, taps, chans), BF16),
+        grad_tx=vm((2, n_sp, taps, chans // 2), BF16), grad_rx=vm((2, n_sp, taps, chans // 2), BF16),
+        all_tx=vm((2, taps, chans // 2), BF16), all_rx=vm((2, n_dp, taps, chans // 2), BF16),
+        last_tx=vm((2, taps, chans // 2), BF16), last_rx=vm((2, n_sp, taps, chans // 2), BF16),
         emb_t=vm((block, chans), F32),
     )
     names = tuple(scratch)
 
     def kernel(*refs):
-        body(n_sp, n_dp, *refs[:12], Scratch(names, refs[12:]))
+        body(n_sp, n_dp, *refs[:13], Scratch(names, refs[13:]))
 
     in_vmem = pl.BlockSpec(memory_space=pltpu.VMEM)
     in_place = pl.BlockSpec(memory_space=pl.ANY)
@@ -658,13 +718,13 @@
             jax.ShapeDtypeStruct((block, hidden), F32),
             jax.ShapeDtypeStruct((hidden, block), F32),
         ),
-        in_specs=[in_vmem] * 2 + [in_place] * 7,
+        in_specs=[in_vmem] * 4 + [in_place] * 6,
         out_specs=(in_vmem,) * 3,
         scratch_shapes=list(scratch.values()),
         compiler_params=pltpu.CompilerParams(
             collective_id=0, has_side_effects=True, vmem_limit_bytes=67043328
         ),
-    )(es, gain_bias, patches, conv_w, emb_w, time_w, up_w, down_w, cotangent[0])
+    )(es, group_norm_gain[None], group_norm_bias[None], planes, conv_w, emb_w, time_w, up_w, down_w, cotangent[0])
 
 
 def solution(mesh):

time: 181 us -> 146 us (0.81)
  Pallas kernels: 162 us -> 138 us
  starting transfers between devices: 6.89 us -> 0 us
  local copies, waits for them, and re-layouts: 8.91 us -> 6.28 us
    pallas_call x1, Pallas kernels: 162 us -> 138 us  [on_device(): pl.pallas_call(kernel, out_shape=(jax.ShapeDtypeStruct(conv_w.shape, F32)...]
    ppermute x1 -> x0, starting transfers between devices: 6.89 us -> none  [on_device(): lax.ppermute(image[:, cols_in - 1, :], 'sp', [(i, i + 1) for i in range(n...]
    slice x9 -> x0, local copies, waits for them, and re-layouts: 2.32 us -> none  [on_device(): padded[row_tap:row_tap + 2 * rows:2, col_tap:col_tap + 2 * cols:2, :]]
    unnamed x16 -> x7, local copies, waits for them, and re-layouts: 5.13 us -> 4.09 us
  transfers between devices with their start and end apart: 1 -> 0, of which waited for: 0 -> 0; matrix products, arithmetic and copies ran while one was open for 1% -> 0% of each run, Pallas kernels for 0% -> 0%
where the time goes in v3:
time: 146 us
  Pallas kernels  138 us (95%)
  local copies, waits for them, and re-layouts  6.28 us (4%)
    pallas_call x1, Pallas kernels, on_device(): pl.pallas_call(kernel, out_shape=(jax.ShapeDtypeStruct(conv_w.shape, F32)...  138 us
    unnamed x7, local copies, waits for them, and re-layouts  4.09 us

profile of v3, /device:TPU:1, one launch (start us, length us, event | category | flops | bytes accessed | tf_op | source)
XLA Modules:
  0.0 146.1 jit_solution(15084972060753112390)
XLA Ops:
  1.3 0.6 broadcast_in_dim.12.refs_0_
  2.0 1.6 %copy.15 = bf16[16,2,8,2,128]{4,2,0,3,1:T(8,128)(2,1)} copy(bf16[16,2,8,2,128]{4,3,2,1,0:T(2,128)(2,1)} %bitcast.10) | data formatting | bytes 262144 | tf_op jit(solution)/shard_map/reshape;squeeze | solution.py:655
  3.5 138.4 %shard_map.121 = (f32[1152,256]{1,0:T(8,128)}, f32[384,384]{1,0:T(8,128)}, f32[384,384]{1,0:T(8,128)}) custom-call(bf16[16,256]{1,0:T(8,128)(2,1)} %broadcast_in_dim.12.refs_0_, f32[1,256]{1,0:T(1,128)} %bitcast.11, f32[1,256]{1,0:T(1,128)} %bitcast.12, bf16[2,2,16,8,128]{4,3,2,1,0:T(8,128)(2,1)} %bitcast.9, bf16[1152,256]{1,0:T(8,128)(2,1)} %refs_4_.1, ...), custom_call_target="tpu_custom_call" | custom-call | tf_op jit(solution)/shard_map/pallas_call | solution.py:714
  142.0 0.0 copy-start.1
  142.0 0.0 copy-start
  142.0 2.5 %copy.20 = f32[1152,256]{1,0:T(8,128)} copy(f32[1152,256]{1,0:T(8,128)} %get-tuple-element.8) | data formatting | bytes 2359296
  144.4 0.0 copy-done.1
  144.4 0.8 copy.21
  145.3 0.0 copy-done
  145.3 0.8 copy.22
  (2 shorter events, 0.1 us)
Async XLA Ops:
  142.0 2.5 %copy-start.1 = (f32[384,384]{1,0:T(8,128)S(1)}, f32[384,384]{1,0:T(8,128)}, u32[]{:S(2)}) copy-start(f32[384,384]{1,0:T(8,128)} %get-tuple-element.9) | copy-start | bytes 1769476
  142.0 3.3 %copy-start = (f32[384,384]{1,0:T(8,128)S(1)}, f32[384,384]{1,0:T(8,128)}, u32[]{:S(2)}) copy-start(f32[384,384]{1,0:T(8,128)} %get-tuple-element.10) | copy-start | bytes 1769476

commit v4 on v3

--- a/solution.py
+++ b/solution.py
@@ -138,6 +138,77 @@
     for name in ("emb", "up"):
         loads[name].start()
 
+    n_row = n_dp // 2
+    row_at = lax.rem(image, n_row)
+    row_first = image - row_at
+    twin = lax.rem(image + n_row, n_dp)
+
+    def in_row(act):
+        others(n_row, row_at, lambda at: act(row_first + at))
+
+    def aim(q):
+        step = lax.rem(q, n_row - 1)
+        away = (1 - q // (n_dp - 2)) * (1 + 2 * step - 3 * (step // 2))
+        swap = lax.rem(q // (n_row - 1) + 1, 2) - q // (n_dp - 1)
+        return swap, lax.rem(row_at + away, n_row)
+
+    def turn(q):
+        swap, at = aim(q)
+        return lax.rem(row_first + swap * n_row, n_dp) + at
+
+    top, low = pl.ds(0, half), pl.ds(half, half)
+    n_late = pixels * 3 // 8
+    late, early = pl.ds(0, n_late), pl.ds(n_late, pixels - n_late)
+    early_top, early_low = pl.ds(n_late, n_late), pl.ds(2 * n_late, pixels - 2 * n_late)
+    routes = {
+        "z": (chip, None, z_peer, z_chip),
+        "e": (chip, None, east, chip_of(west_col, far)),
+        "w": (chip, None, west, chip_of(east_col, far)),
+        "ez": (z_chip, early, east, chip_of(west_col, 1 - far)),
+        "wz": (z_chip, early, west, chip_of(east_col, 1 - far)),
+        "ee": (chip_of(west_col, far), top, east, chip_of(over_col, far)),
+        "ww": (chip_of(east_col, far), low, west, chip_of(over_col, far)),
+        "eez": (chip_of(west_col, 1 - far), early_top, east, chip_of(over_col, 1 - far)),
+        "wwz": (chip_of(east_col, 1 - far), early_low, west, chip_of(over_col, 1 - far)),
+        "ze": (chip_of(west_col, far), late, z_peer, chip_of(west_col, 1 - far)),
+        "zw": (chip_of(east_col, far), late, z_peer, chip_of(east_col, 1 - far)),
+        "zo": (chip_of(over_col, far), late, z_peer, chip_of(over_col, 1 - far)),
+    }
+    order = {name: index for index, name in enumerate(routes)}
+
+    def cot_copy(name, p, arriving=False):
+        mine, part, to, theirs = routes[name]
+        which = theirs if arriving else mine
+        ref = s.cot.at[p, which] if part is None else s.cot.at[p, which, part, :]
+        at = order[name] * n_dp + p
+        return send(ref, ref, s.cot_sem, at, at, sp=to)
+
+    def across(q):
+        cot_copy("z", turn(q)).start()
+
+    def beside(q):
+        p = turn(q)
+        cot_copy("e", p).start()
+        cot_copy("w", p).start()
+
+    def relay(q, steps):
+        p = turn(q)
+        for name, then in steps:
+            cot_copy(name, p, True).wait_recv()
+            for onward in then:
+                cot_copy(onward, p).start()
+
+    def relay_near(q):
+        relay(q, (("z", ("ez", "wz")), ("e", ("ee", "ze")), ("w", ("ww", "zw"))))
+
+    def relay_far(q):
+        relay(q, (("ez", ("eez",)), ("wz", ("wwz",)), ("ee", ("zo",))))
+
+    def landed(q):
+        p = turn(q)
+        for name in ("ww", "eez", "wwz", "ze", "zw", "zo"):
+            cot_copy(name, p, True).wait_recv()
+
     for parity in range(2):
         s.rim_tx[parity] = planes[parity, 1].astype(F32)[:, cols - 1, :].astype(BF16)
 
@@ -151,6 +222,11 @@
     @pl.when(me < n_sp - 1)
     def _():
         rim_copy.start()
+
+    every(n_dp, lambda p: cot_load(p).wait())
+    for q in range(2):
+        across(q)
+        beside(q)
 
     first_column = lax.broadcasted_iota(jnp.int32, (rows, cols, in_chans), 1) == 0
 
@@ -190,58 +266,10 @@
         return send(s.stat_tx, s.stat_rx.at[p], s.stat_sem, p, p, sp=p)
 
     others(n_sp, me, lambda p: stat_copy(p).start())
-
-    every(n_dp, lambda p: cot_load(p).wait())
-
-    def turn(q):
-        return lax.rem(image + 1 + q, n_dp)
-
-    top, low = pl.ds(0, half), pl.ds(half, half)
-    routes = {
-        "z": (chip, None, z_peer, z_chip),
-        "e": (chip, None, east, chip_of(west_col, far)),
-        "w": (chip, None, west, chip_of(east_col, far)),
-        "ez": (z_chip, None, east, chip_of(west_col, 1 - far)),
-        "wz": (z_chip, None, west, chip_of(east_col, 1 - far)),
-        "ee": (chip_of(west_col, far), top, east, chip_of(over_col, far)),
-        "ww": (chip_of(east_col, far), low, west, chip_of(over_col, far)),
-        "eez": (chip_of(west_col, 1 - far), top, east, chip_of(over_col, 1 - far)),
-        "wwz": (chip_of(east_col, 1 - far), low, west, chip_of(over_col, 1 - far)),
-    }
-    order = {name: index for index, name in enumerate(routes)}
-
-    def cot_copy(name, p, arriving=False):
-        mine, part, to, theirs = routes[name]
-        which = theirs if arriving else mine
-        ref = s.cot.at[p, which] if part is None else s.cot.at[p, which, part, :]
-        at = order[name] * n_dp + p
-        return send(ref, ref, s.cot_sem, at, at, sp=to)
-
-    def own(q):
-        p = turn(q)
-        for name in ("z", "e", "w"):
-            cot_copy(name, p).start()
-
-    def relay(q, steps):
-        p = turn(q)
-        for name, then in steps:
-            cot_copy(name, p, True).wait_recv()
-            for onward in then:
-                cot_copy(onward, p).start()
-
-    def relay_near(q):
-        relay(q, (("z", ("ez", "wz")), ("e", ("ee",)), ("w", ("ww",))))
-
-    def relay_far(q):
-        relay(q, (("ez", ("eez",)), ("wz", ("wwz",))))
-
-    def landed(q):
-        p = turn(q)
-        for name in ("ee", "ww", "eez", "wwz"):
-            cot_copy(name, p, True).wait_recv()
-
-    own(0)
-    own(1)
+    across(2)
+    across(3)
+    relay_near(0)
+    beside(2)
 
     every(n_dp, lambda p: down_load(p).wait())
     my_down, its_down = s.gated.at[:, my_rows], s.gated.at[:, its_rows]
@@ -283,9 +311,11 @@
         return send(s.act_tx.at[lax.rem(p, 2)], s.act_rx.at[source], s.act_sem, p, source, sp=p)
 
     others(n_sp, me, lambda p: act_copy(p, me).start())
-    own(2)
-    relay_near(0)
-    own(3)
+    for q in range(4, n_dp):
+        across(q)
+    relay_near(1)
+    beside(3)
+    relay_far(0)
 
     loads["emb"].wait()
     loads["up"].wait()
@@ -320,9 +350,9 @@
     mix_copy.start()
     off_copy = send(s.offsets.at[:, my_cols], s.offsets.at[:, my_cols], s.pair_sem, 2, 2, sp=sibling)
     off_copy.start()
-    relay_near(1)
-    relay_far(0)
-    own(4)
+    relay_near(2)
+    beside(4)
+    relay_far(1)
 
     down_from = send(its_down, its_down, s.pair_sem, 0, 0, sp=sibling)
     down_copy.wait_send()
@@ -366,16 +396,29 @@
         s.token_rstd[i] = jnp.broadcast_to(token_rstd, (pixels, 128))
         s.dhid[i] = jnp.zeros_like(slope)
 
-    relay_near(2)
-    relay_far(1)
+    relay_near(3)
+    beside(5)
+    relay_far(2)
     every(n_chip, forward)
     s.patches_t[...] = s.patches[...].astype(F32).T.astype(BF16)
 
     def sib_copy(p):
         return send(s.sib_tx.at[p], s.sib_rx.at[p], s.sib_sem, p, p, sp=sibling)
 
-    def down_out(p, source, to):
-        return send(s.gd_tx.at[p], s.gd_rx.at[source], s.gd_sem, p, source, dp=to)
+    def down_out(q):
+        swap, at = aim(q)
+        p, slot = turn(q), swap * n_row + row_at
+        return send(s.gd_tx.at[p], s.gd_rx.at[slot], s.gd_sem, p, slot, dp=row_first + at)
+
+    def down_from(swap, act):
+        def one(p):
+            slot = swap * n_row + lax.rem(p, n_row)
+            send(s.gd_tx.at[p], s.gd_rx.at[slot], s.gd_sem, p, slot, dp=p).wait_recv()
+            act(s.gd_rx[slot].astype(F32))
+
+        in_row(one)
+
+    twin_out = send(s.gd_tx.at[twin], s.gd_twin, s.gd_sem, n_dp, n_dp, dp=twin)
 
     def block_of(q):
         p = turn(q)
@@ -399,22 +442,36 @@
 
     def hand_over(q):
         p, total = whole(q)
-        s.gd_tx[p] = total.astype(BF16)
-        down_out(p, image, p).start()
+
+        @pl.when(q < n_dp - 2)
+        def _():
+            s.gd_tx[p] = total.astype(BF16)
+            down_out(q).start()
+
+        @pl.when(q == n_dp - 2)
+        def _():
+            out_down[...] = total
+
+            def add(value):
+                out_down[...] += value
+
+            down_from(1, add)
+            s.gd_tx[twin] = out_down[...].astype(BF16)
+            twin_out.start()
 
     @pl.loop(0, n_dp)
     def _(q):
-        @pl.when(q + 5 < n_dp)
+        @pl.when(q + 6 < n_dp)
         def _():
-            own(q + 5)
+            beside(q + 6)
+
+        @pl.when(q + 4 < n_dp)
+        def _():
+            relay_near(q + 4)
 
         @pl.when(q + 3 < n_dp)
         def _():
-            relay_near(q + 3)
-
-        @pl.when(q + 2 < n_dp)
-        def _():
-            relay_far(q + 2)
+            relay_far(q + 3)
 
         @pl.when(q > 0)
         def _():
@@ -478,13 +535,6 @@
 
     def side_copy(p, source):
         return send(s.side_tx.at[p], s.side_rx.at[source], s.side_sem, p, source, dp=p)
-
-    n_row = n_dp // 2
-    row_first = image // n_row * n_row
-    twin = lax.rem(image + n_row, n_dp)
-
-    def in_row(act):
-        others(n_row, image - row_first, lambda at: act(row_first + at))
 
     def forward_copy(p):
         at = lax.rem(p + n_row, n_dp)
@@ -571,12 +621,12 @@
         s.last_rx[h, me] = s.last_tx[h]
         others(n_sp, me, lambda p: last_copy(h, p, me).start())
 
-    others(n_dp, image, lambda p: down_out(p, p, p).wait_recv())
-
-    def add_down(p):
-        out_down[...] += s.gd_rx[p].astype(F32)
-
-    others(n_dp, image, add_down)
+    def add_down(value):
+        out_down[...] += value
+
+    down_from(0, add_down)
+    twin_out.wait_recv()
+    add_down(s.gd_twin[...].astype(F32))
 
     in_row(lambda p: q_copy(p, p).wait_recv())
     in_row(lambda p: q_copy(p, lax.rem(p + n_row, n_dp)).wait_recv())
@@ -624,12 +674,15 @@
     others(n_sp, me, left)
 
     def left_dp(p):
-        for copy in (down_out(p, image, p), q_copy(p, image), side_copy(p, image)):
+        for copy in (q_copy(p, image), side_copy(p, image)):
             copy.wait_send()
         for h in range(n_half):
             all_copy(h, p, image).wait_send()
 
     others(n_dp, image, left_dp)
+
+    every(n_dp - 2, lambda q: down_out(q).wait_send())
+    twin_out.wait_send()
 
     def left_block(p):
         sib_copy(p).wait_send()
@@ -671,8 +724,8 @@
     scratch = dict(
         load=pltpu.SemaphoreType.DMA((8 + 2 * n_dp + time_w.shape[1] // 1024,)),
         stat_sem=dma(n_sp), act_sem=dma(n_sp), part_sem=dma(n_sp), stat2_sem=dma(n_sp),
-        grad_sem=dma(2 * n_sp), last_sem=dma(2 * n_sp), cot_sem=dma(9 * n_dp), pair_sem=dma(8),
-        sib_sem=dma(n_dp), gd_sem=dma(n_dp), q_sem=dma(n_dp), side_sem=dma(n_dp), all_sem=dma(2 * n_dp),
+        grad_sem=dma(2 * n_sp), last_sem=dma(2 * n_sp), cot_sem=dma(12 * n_dp), pair_sem=dma(8),
+        sib_sem=dma(n_dp), gd_sem=dma(n_dp + 1), q_sem=dma(n_dp), side_sem=dma(n_dp), all_sem=dma(2 * n_dp),
         patches=vm((pixels, 9 * in_chans), BF16), rim_tx=vm((2, rows, in_chans), BF16),
         rim_rx=vm((2, rows, in_chans), BF16), conv=vm(conv_w.shape, BF16), emb=vm(emb_w.shape, BF16),
         time=vm((time_w.shape[1] // 1024, time_w.shape[0], 1024), BF16), up=vm(up_w.shape, BF16),
@@ -692,7 +745,7 @@
         patches_t=vm((9 * in_chans, pixels), BF16),
         sib_tx=vm((n_dp, hidden, block), BF16), sib_rx=vm((n_dp, hidden, block), BF16),
         gd_own=vm((2, hidden, block), F32), gd_tx=vm((n_dp, hidden, block), BF16),
-        gd_rx=vm((n_dp, hidden, block), BF16), du_sum=vm((8, 2 * hidden), F32),
+        gd_rx=vm((n_dp, hidden, block), BF16), gd_twin=vm((hidden, block), BF16), du_sum=vm((8, 2 * hidden), F32),
         du=vm((tokens, 2 * hidden), BF16), part_tx=vm((n_sp, half, chans), BF16),
         part_rx=vm((n_sp, half, chans), BF16), pairs=vm((chans, 2 * hidden), F32),
         pair_tx=vm((chans, hidden), BF16), pair_rx=vm((chans, hidden), BF16),

time: 146 us -> 130 us (0.89)
  Pallas kernels: 138 us -> 122 us
    pallas_call x1, Pallas kernels: 138 us -> 122 us  [on_device(): pl.pallas_call(kernel, out_shape=(jax.ShapeDtypeStruct(conv_w.shape, F32)...]
where the time goes in v4:
time: 130 us; the launch traced here: 129 us
  Pallas kernels  122 us (94%)
  local copies, waits for them, and re-layouts  6.28 us (5%)
  between operations  1.31 us (1%)
    pallas_call x1, Pallas kernels, on_device(): pl.pallas_call(kernel, out_shape=(jax.ShapeDtypeStruct(conv_w.shape, F32)...  122 us
    unnamed x7, local copies, waits for them, and re-layouts  4.09 us

profile of v4, /device:TPU:1, one launch (start us, length us, event | category | flops | bytes accessed | tf_op | source)
XLA Modules:
  0.0 129.3 jit_solution(16400884430762389726)
XLA Ops:
  1.3 0.6 broadcast_in_dim.12.refs_0_
  2.0 1.6 %copy.15 = bf16[16,2,8,2,128]{4,2,0,3,1:T(8,128)(2,1)} copy(bf16[16,2,8,2,128]{4,3,2,1,0:T(2,128)(2,1)} %bitcast.10) | data formatting | bytes 262144 | tf_op jit(solution)/shard_map/reshape;squeeze | solution.py:708
  3.5 121.7 %shard_map.121 = (f32[1152,256]{1,0:T(8,128)}, f32[384,384]{1,0:T(8,128)}, f32[384,384]{1,0:T(8,128)}) custom-call(bf16[16,256]{1,0:T(8,128)(2,1)} %broadcast_in_dim.12.refs_0_, f32[1,256]{1,0:T(1,128)} %bitcast.11, f32[1,256]{1,0:T(1,128)} %bitcast.12, bf16[2,2,16,8,128]{4,3,2,1,0:T(8,128)(2,1)} %bitcast.9, bf16[1152,256]{1,0:T(8,128)(2,1)} %refs_4_.1, ...), custom_call_target="tpu_custom_call" | custom-call | tf_op jit(solution)/shard_map/pallas_call | solution.py:767
  125.2 0.0 copy-start.1
  125.2 0.0 copy-start
  125.2 2.5 %copy.20 = f32[1152,256]{1,0:T(8,128)} copy(f32[1152,256]{1,0:T(8,128)} %get-tuple-element.8) | data formatting | bytes 2359296
  127.7 0.0 copy-done.1
  127.7 0.8 copy.21
  128.5 0.0 copy-done
  128.5 0.8 copy.22
  (2 shorter events, 0.1 us)
Async XLA Ops:
  125.2 2.5 %copy-start.1 = (f32[384,384]{1,0:T(8,128)S(1)}, f32[384,384]{1,0:T(8,128)}, u32[]{:S(2)}) copy-start(f32[384,384]{1,0:T(8,128)} %get-tuple-element.9) | copy-start | bytes 1769476
  125.2 3.3 %copy-start = (f32[384,384]{1,0:T(8,128)S(1)}, f32[384,384]{1,0:T(8,128)}, u32[]{:S(2)}) copy-start(f32[384,384]{1,0:T(8,128)} %get-tuple-element.10) | copy-start | bytes 1769476

commit v5 on v4

--- a/solution.py
+++ b/solution.py
@@ -224,9 +224,9 @@
         rim_copy.start()
 
     every(n_dp, lambda p: cot_load(p).wait())
-    for q in range(2):
-        across(q)
-        beside(q)
+    across(0)
+    across(1)
+    beside(0)
 
     first_column = lax.broadcasted_iota(jnp.int32, (rows, cols, in_chans), 1) == 0
 
@@ -268,6 +268,7 @@
     others(n_sp, me, lambda p: stat_copy(p).start())
     across(2)
     across(3)
+    beside(1)
     relay_near(0)
     beside(2)
 
@@ -568,6 +569,9 @@
 
     others(n_sp, me, lambda p: stat2_copy(p, me).start())
 
+    q_copy(twin, twin).wait_recv()
+    in_row(lambda p: forward_copy(p).start())
+
     others(n_sp, me, lambda p: stat2_copy(p, p).wait_recv())
     first, second = group_sums(s.stat2_rx)
     dz = (s.rstd[0:1, :] * (s.slope0[...] - first - s.z[...] * second)).astype(BF16)
@@ -611,9 +615,6 @@
         s.all_tx[h] = slots(s.grad_rx, h, n_sp).astype(BF16)
         s.all_rx[h, image] = s.all_tx[h]
         others(n_dp, image, lambda p: all_copy(h, p, image).start())
-
-    q_copy(twin, twin).wait_recv()
-    in_row(lambda p: forward_copy(p).start())
 
     for h in range(n_half):
         others(n_dp, image, lambda p: all_copy(h, p, p).wait_recv())

time: 130 us -> 127 us (0.977)
  Pallas kernels: 122 us -> 119 us
    pallas_call x1, Pallas kernels: 122 us -> 119 us  [on_device(): pl.pallas_call(kernel, out_shape=(jax.ShapeDtypeStruct(conv_w.shape, F32)...]
where the time goes in v5:
time: 127 us; the launch traced here: 126 us
  Pallas kernels  119 us (94%)
  local copies, waits for them, and re-layouts  6.28 us (5%)
  between operations  1.31 us (1%)
    pallas_call x1, Pallas kernels, on_device(): pl.pallas_call(kernel, out_shape=(jax.ShapeDtypeStruct(conv_w.shape, F32)...  119 us
    unnamed x7, local copies, waits for them, and re-layouts  4.09 us

profile of v5, /device:TPU:1, one launch (start us, length us, event | category | flops | bytes accessed | tf_op | source)
XLA Modules:
  0.0 126.5 jit_solution(5281813386433956483)
XLA Ops:
  1.3 0.6 broadcast_in_dim.12.refs_0_
  2.0 1.6 %copy.15 = bf16[16,2,8,2,128]{4,2,0,3,1:T(8,128)(2,1)} copy(bf16[16,2,8,2,128]{4,3,2,1,0:T(2,128)(2,1)} %bitcast.10) | data formatting | bytes 262144 | tf_op jit(solution)/shard_map/reshape;squeeze | solution.py:709
  3.5 118.8 %shard_map.121 = (f32[1152,256]{1,0:T(8,128)}, f32[384,384]{1,0:T(8,128)}, f32[384,384]{1,0:T(8,128)}) custom-call(bf16[16,256]{1,0:T(8,128)(2,1)} %broadcast_in_dim.12.refs_0_, f32[1,256]{1,0:T(1,128)} %bitcast.11, f32[1,256]{1,0:T(1,128)} %bitcast.12, bf16[2,2,16,8,128]{4,3,2,1,0:T(8,128)(2,1)} %bitcast.9, bf16[1152,256]{1,0:T(8,128)(2,1)} %refs_4_.1, ...), custom_call_target="tpu_custom_call" | custom-call | tf_op jit(solution)/shard_map/pallas_call | solution.py:768
  122.4 0.0 copy-start.1
  122.4 0.0 copy-start
  122.4 2.5 %copy.20 = f32[1152,256]{1,0:T(8,128)} copy(f32[1152,256]{1,0:T(8,128)} %get-tuple-element.8) | data formatting | bytes 2359296
  124.9 0.0 copy-done.1
  124.9 0.8 copy.21
  125.7 0.0 copy-done
  125.7 0.8 copy.22
  (2 shorter events, 0.1 us)
Async XLA Ops:
  122.4 2.5 %copy-start.1 = (f32[384,384]{1,0:T(8,128)S(1)}, f32[384,384]{1,0:T(8,128)}, u32[]{:S(2)}) copy-start(f32[384,384]{1,0:T(8,128)} %get-tuple-element.9) | copy-start | bytes 1769476
  122.4 3.3 %copy-start = (f32[384,384]{1,0:T(8,128)S(1)}, f32[384,384]{1,0:T(8,128)}, u32[]{:S(2)}) copy-start(f32[384,384]{1,0:T(8,128)} %get-tuple-element.10) | copy-start | bytes 1769476
